TPU v7x, 256 devices: a whole 4x4x8 slice. The times are simulated.
256 devices in a mesh: grp: 4 (over x), own: 64 (over y, z, core).
Axes of the slice: x: 4, y: 4, z: 8, core: 2. Of those that a mesh axis runs over, the one named last changes fastest.
Arguments:
- grad_parts: float32 [4, 64, 4, 64, 16, 2, 128], P('grp', 'own'), may hold values from -6 to 6
- block_ids: int32 [64, 4, 64, 16], P('own'), may hold values from 0 to 1023, as said below
- block_counts: int32 [64, 4, 64], P('own'), may hold values from 0 to 16, as said below
- params: float32 [8, 32768, 2, 128], P(None, ('grp', 'own')), may hold values from -4 to 4
- first_moment: float32 [8, 32768, 2, 128], P(None, ('grp', 'own')), may hold values from -2 to 2
- second_moment: float32 [8, 32768, 2, 128], P(None, ('grp', 'own')), may hold values from 0.0001 to 0.03
Outputs:
- new_params: float32 [8, 32768, 2, 128], P(None, ('grp', 'own'))
- new_first: float32 [8, 32768, 2, 128], P(None, ('grp', 'own'))
- new_second: float32 [8, 32768, 2, 128], P(None, ('grp', 'own'))
Inputs may be any that keep to these rules, and one draw needn't show every extreme that they name: `block_ids`: within one row (fixed group and destination) the 16 block numbers are distinct; numbers in slots beyond the count are arbitrary but in range. `block_counts`: some destination device gets 16 used slots from every ray group.
All inputs are finite; a program needn't handle non-finite values.
Results may differ from a plain program's by a relative error of at most 0.00002.
Values sent between devices are 32-bit elements; how exact they have to be, the bound alone decides.
No kernel may reach another device: no remote copies, remote signals or barrier semaphores. Data moves between devices by JAX's collectives and lax.ppermute only.
A program may use at most 64 MiB of HBM per device.

v0:
```python
import math

import jax
import jax.numpy as jnp
from jax import lax
from jax.sharding import Mesh
from jax.sharding import PartitionSpec as P

OWN = ("own_0", "own_1", "own_2")
GRP_OWN = ("grp", "own_0", "own_1", "own_2")


def sent_together(arrays, axis, split_dim, concat_dim, along):
    widths = [math.prod(a.shape[along:]) for a in arrays]
    both = jnp.concatenate(
        [a.reshape(*a.shape[:along], w) for a, w in zip(arrays, widths)], axis=along
    )
    result = lax.all_to_all(both, axis, split_axis=split_dim, concat_axis=concat_dim, tiled=True)
    pieces = jnp.split(result, [sum(widths[:k]) for k in range(1, len(widths))], axis=along)
    return tuple(
        (b.reshape(*result.shape[:along], *a.shape[along:]) for a, b in zip(arrays, pieces))
    )


def over_axes(value, axes):
    for axis in axes:
        value = lax.psum(value, axis)
    return value


def shards(grad_parts, block_ids, block_counts, params, first_moment, second_moment):
    member = lax.axis_index("grp")
    partial_value = grad_parts[0, 0]
    listing = block_ids[0]
    tallies = block_counts[0]
    share = lax.psum_scatter(partial_value, "grp", scatter_dimension=0, tiled=True)[0]
    send_ids = lax.dynamic_index_in_dim(listing, member, 0, keepdims=False)
    send_counts = lax.dynamic_index_in_dim(tallies, member, 0, keepdims=False)
    summed, mine_ids, mine_counts = (
        lax.all_to_all(share, OWN, split_axis=0, concat_axis=0, tiled=True),
        *sent_together((send_ids, send_counts), OWN, 0, 0, 1),
    )
    slot_count = summed.shape[1]
    width = summed.shape[2] * summed.shape[3]
    local_blocks = params.shape[0] * params.shape[1]
    valid = jnp.arange(slot_count, dtype=jnp.int32)[None, :] < mine_counts[:, None]
    rows = summed.reshape(-1, width) * valid.reshape(-1, 1).astype(jnp.float32)
    target = mine_ids.reshape(-1).astype(jnp.int32)
    dense = jax.ops.segment_sum(rows, target, num_segments=local_blocks)
    hits = (
        jax.ops.segment_sum(valid.reshape(-1).astype(jnp.int32), target, num_segments=local_blocks)
        > 0
    )
    square = jnp.sum(dense * dense)
    touched = jnp.sum(hits.astype(jnp.float32))
    square, touched = (over_axes(square, GRP_OWN), over_axes(touched, GRP_OWN))
    rms = jnp.sqrt(square / (touched * width) + 1e-06)
    scale = jnp.minimum(jnp.float32(1.0), 0.5 / rms)
    clipped = scale * dense
    old_p = params.reshape(local_blocks, width)
    old_m = first_moment.reshape(local_blocks, width)
    old_v = second_moment.reshape(local_blocks, width)
    mask = hits[:, None]
    new_m = jnp.where(mask, 0.9 * old_m + 0.1 * clipped, old_m)
    new_v = jnp.where(mask, 0.99 * old_v + 0.01 * clipped * clipped, old_v)
    stepped = old_p - 0.01 * (new_m / (1.0 - 0.9**8)) / (jnp.sqrt(new_v / (1.0 - 0.99**8)) + 1e-08)
    new_p = jnp.where(mask, stepped, old_p)
    shape = params.shape
    return (new_p.reshape(shape), new_m.reshape(shape), new_v.reshape(shape))


def solution(mesh):
    split = Mesh(
        mesh.devices.reshape(mesh.shape["grp"], 4, 8, 2), ("grp", "own_0", "own_1", "own_2")
    )
    in_specs = (
        P("grp", OWN, None, None, None, None, None),
        P(OWN, None, None, None),
        P(OWN, None, None),
        P(None, GRP_OWN, None, None),
        P(None, GRP_OWN, None, None),
        P(None, GRP_OWN, None, None),
    )
    out_specs = (
        P(None, GRP_OWN, None, None),
        P(None, GRP_OWN, None, None),
        P(None, GRP_OWN, None, None),
    )
    return jax.shard_map(
        shards, mesh=split, in_specs=in_specs, out_specs=out_specs, check_vma=False
    )
```

profile of v0, /device:TPU:1, one launch (start us, length us, event | category | flops | bytes accessed | tf_op | source)
XLA Modules:
  0.0 168.8 jit_solution(18409456818328872322)
XLA Ops:
  7.2 0.0 copy-start
  7.2 0.0 reduce-scatter.2.cloned.1.call-start
  7.2 4.6 %copy.34 = f32[1,1,4,64,16,2,128]{6,4,5,3,2,1,0:T(8,128)} copy(f32[1,1,4,64,16,2,128]{6,5,4,3,2,1,0:T(2,128)} %param.6) | data formatting | bytes 8388608 | tf_op args[0]
  11.8 0.0 reduce-scatter.2.cloned.1.call-update
  11.8 0.7 dynamic-slice_bitcast_fusion.1
  12.5 0.0 copy-done
  12.5 0.1 copy.17
  12.6 22.2 %all_to_all.17 = s32[64,1,17]{2,1,0:T(1,128)S(1)} all-to-all(s32[64,1,17]{2,1,0:T(1,128)S(1)} %bitcast.46), channel_id=1, replica_groups=mesh['grp'=4,'own_0'=4,'own_1'=8,'own_2'=2] {'own_0','own_1','own_2'}, dimensions={0} | all-to-all | bytes 8704 | tf_op jit(solution)/shard_map/all_to_all | solution.py:18
  34.9 30.2 %reduce-scatter.2.cloned.1.call-done = f32[1,64,16,2,128]{4,2,3,1,0:T(8,128)} async-done(((f32[4,64,16,2,128]{4,2,3,1,0:T(8,128)}), f32[1,64,16,2,128]{4,2,3,1,0:T(8,128)}) %reduce-scatter.2.cloned.1.call-update) | async-done | bytes 1048592 | tf_op jit(solution)/shard_map/reduce_scatter | solution.py:36
  65.1 10.8 %all-to-all-start.1 = ((f32[64,16,2,128]{3,1,2,0:T(8,128)}), f32[64,16,2,128]{3,1,2,0:T(8,128)S(1)}, u32[]{:S(2)}, u32[]{:S(2)}) async-start(f32[64,16,2,128]{3,1,2,0:T(8,128)} %bitcast.40), calls=%async_computation.2 | async-start | bytes 2097152 | tf_op jit(solution)/shard_map/all_to_all | solution.py:40
  75.8 0.1 reshape.73
  75.9 0.2 slice_reduce_fusion
  76.1 0.1 fusion.8
  76.2 0.1 reshape.70
  76.2 0.1 reshape.75
  76.3 7.6 %scatter_custom_fusion = s32[1024]{0:T(1024)S(1)} fusion(s32[1024]{0:T(1024)S(1)} %reshape.73, s32[1024]{0:T(1024)S(1)} %reshape.75, s32[]{:T(128)} %constant.16.clone.1), kind=kCustom, calls=%fused_computation.25 | custom fusion | flops 1024 | bytes 4100 | tf_op jit(solution)/shard_map/scatter-add | solution.py:51
  83.9 0.6 convert_reduce_fusion
  84.5 19.8 %all-to-all-done.1 = f32[64,16,2,128]{3,1,2,0:T(8,128)S(1)} async-done(((f32[64,16,2,128]{3,1,2,0:T(8,128)}), f32[64,16,2,128]{3,1,2,0:T(8,128)S(1)}, u32[]{:S(2)}, u32[]{:S(2)}) %all-to-all-start.1) | async-done | bytes 1048608 | tf_op jit(solution)/shard_map/all_to_all | solution.py:40
  104.4 0.5 copy.19
  104.9 7.0 %scatter_custom_fusion.1 = f32[1024,256]{1,0:T(8,128)S(1)} fusion(s32[1024]{0:T(1024)S(1)} %reshape.73, f32[128,8,2,128]{3,2,1,0:T(2,128)S(1)} %bitcast.39, f32[1024]{0:T(1024)S(1)} %reshape.70, f32[]{:T(128)} %constant.13.clone.1), kind=kCustom, calls=%fused_computation.9 | custom fusion | flops 524288 | bytes 2101252 | tf_op jit(solution)/shard_map/scatter-add | solution.py:49
  111.9 0.9 multiply_reduce_fusion
  112.7 7.2 %all-reduce.2 = (f32[]{:T(128)}, f32[]{:T(128)}) all-reduce(f32[]{:T(128)} %multiply_reduce_fusion, f32[]{:T(128)} %get-tuple-element.14), channel_id=1, replica_groups=mesh['grp'=4,'own_0'=4,'own_1'=8,'own_2'=2] {'grp'}, use_global_device_ids=true, to_apply=%region_4.5 | all-reduce | flops 2 | bytes 16 | tf_op jit(solution)/shard_map/psum | solution.py:27
  119.9 9.5 %all-reduce.1 = (f32[]{:T(128)}, f32[]{:T(128)}) all-reduce(f32[]{:T(128)} %get-tuple-element.7, f32[]{:T(128)} %get-tuple-element.8), channel_id=1, replica_groups=mesh['grp'=4,'own_0'=4,'own_1'=8,'own_2'=2] {'own_0'}, use_global_device_ids=true, to_apply=%region_5.6 | all-reduce | flops 2 | bytes 16 | tf_op jit(solution)/shard_map/psum | solution.py:27
  129.4 11.4 %all-reduce = (f32[]{:T(128)}, f32[]{:T(128)}) all-reduce(f32[]{:T(128)} %get-tuple-element.5, f32[]{:T(128)} %get-tuple-element.6), channel_id=1, replica_groups=mesh['grp'=4,'own_0'=4,'own_1'=8,'own_2'=2] {'own_1'}, use_global_device_ids=true, to_apply=%region_6.7 | all-reduce | flops 2 | bytes 16 | tf_op jit(solution)/shard_map/psum | solution.py:27
  140.8 10.4 %all-reduce.3 = (f32[]{:T(128)}, f32[]{:T(128)}) all-reduce(f32[]{:T(128)} %get-tuple-element.3, f32[]{:T(128)} %get-tuple-element.4), channel_id=1, replica_groups=mesh['grp'=4,'own_0'=4,'own_1'=8,'own_2'=2] {'own_2'}, use_global_device_ids=true, to_apply=%region_7.8 | all-reduce | flops 2 | bytes 16 | tf_op jit(solution)/shard_map/psum | solution.py:27
  152.6 3.7 %subtract_select_fusion = (f32[1024,256]{1,0:T(8,128)}, f32[1024,256]{1,0:T(8,128)S(1)}, f32[1024,256]{1,0:T(8,128)S(1)}) fusion(f32[128,8,2,128]{3,2,1,0:T(2,128)} %bitcast.41, pred[1024]{0:T(1024)(128)(4,1)S(1)} %get-tuple-element.15, f32[1024,256]{1,0:T(8,128)S(1)} %scatter_custom_fusion.1, f32[]{:T(128)S(6)} %min_shard_map.3, ...), kind=kLoop, calls=%fused_computation.3 | loop fusion | flops 4194304 | bytes 7341060 | tf_op jit(solution)/shard_map/jit(_where)/select_n | solution.py:67
  156.3 2.7 %reshape.66 = f32[8,128,2,128]{3,2,1,0:T(2,128)} reshape(f32[1024,256]{1,0:T(8,128)} %get-tuple-element.11) | data formatting | bytes 2097152 | tf_op jit(solution)/shard_map/reshape | solution.py:69
  159.0 1.5 reshape.67
  160.5 1.5 reshape.68
  (2 shorter events, 0.0 us)
Async XLA Ops:
  7.2 5.4 %copy-start = (s32[1,4,64,16]{2,3,1,0:T(8,128)S(1)}, s32[1,4,64,16]{2,3,1,0:T(8,128)}, u32[]{:S(2)}) copy-start(s32[1,4,64,16]{2,3,1,0:T(8,128)} %param.7) | copy-start | bytes 49156
  7.2 57.9 %reduce-scatter.2.cloned.1.call-start = ((), (), s32[]{:S(2)}) async-start(), calls=%async_computation.3 | async-start | bytes 5242880 | tf_op jit(solution)/shard_map/reduce_scatter | solution.py:36
  65.1 39.3 %all-to-all-start.1 = ((f32[64,16,2,128]{3,1,2,0:T(8,128)}), f32[64,16,2,128]{3,1,2,0:T(8,128)S(1)}, u32[]{:S(2)}, u32[]{:S(2)}) async-start(f32[64,16,2,128]{3,1,2,0:T(8,128)} %bitcast.40), calls=%async_computation.2 | async-start | bytes 2097152 | tf_op jit(solution)/shard_map/all_to_all | solution.py:40
Sparse Core Ops, SparseCore 0:
  11.9 53.0 reduce-scatter.1
where the time goes:
time: 169 us
  blocking collectives  60.7 us (36%)
  waiting for transfers between devices  50 us (30%)
  other arithmetic  19.8 us (12%)
  between operations  15.4 us (9%)
  local copies, waits for them, and re-layouts  12 us (7%)
  starting transfers between devices  10.8 us (6%)
    psum x4, blocking collectives, over_axes(): value = lax.psum(value, axis)  38.5 us
    reduce_scatter x1, waiting for transfers between devices, shards(): lax.psum_scatter(partial_value, 'grp', scatter_dimension=0, tiled=True)[0]  30.2 us
    all_to_all x1, blocking collectives, sent_together(): lax.all_to_all(both, axis, split_axis=split_dim, concat_axis=concat_dim,...  22.2 us
    all_to_all x1, waiting for transfers between devices, shards(): lax.all_to_all(share, OWN, split_axis=0, concat_axis=0, tiled=True)  19.8 us
    all_to_all x1, starting transfers between devices, shards(): lax.all_to_all(share, OWN, split_axis=0, concat_axis=0, tiled=True)  10.8 us
    scatter-add x1, other arithmetic, shards(): jax.ops.segment_sum(valid.reshape(-1).astype(jnp.int32), target, num_segm...  7.62 us
    scatter-add x1, other arithmetic, shards(): dense = jax.ops.segment_sum(rows, target, num_segments=local_blocks)  6.96 us
    reshape x3, local copies, waits for them, and re-layouts, shards(): return (new_p.reshape(shape), new_m.reshape(shape), new_v.reshape(shape))  5.68 us
  transfers between devices with their start and end apart: 2, of which 2 were waited for; matrix products, arithmetic and copies ran while one was open for 6% of the time, Pallas kernels for 0%

commit v1 on v0

v1 whole, which is shorter than its diff:
```python
import functools

import jax
import jax.numpy as jnp
from jax import lax
from jax.experimental import pallas as pl
from jax.experimental.pallas import tpu as pltpu
from jax.sharding import Mesh
from jax.sharding import PartitionSpec as P


OWN = ("own_0", "own_1", "own_2")
GRP_OWN = ("grp", "own_0", "own_1", "own_2")
CHUNKS = (8, 8)
STEPS = 4
f32 = jnp.float32
ANY = pl.BlockSpec(memory_space=pl.ANY)
VMEM = pl.BlockSpec(memory_space=pltpu.VMEM)
SMEM = pl.BlockSpec(memory_space=pltpu.SMEM)


def kernel_call(body, outs, ins, out_specs, scratch=(), aliases=None, moved=1 << 20):
    return pl.pallas_call(
        body,
        out_shape=outs,
        in_specs=ins,
        out_specs=out_specs,
        scratch_shapes=list(scratch),
        input_output_aliases=aliases or {},
        compiler_params=pltpu.CompilerParams(vmem_limit_bytes=16 << 20),
        cost_estimate=pl.CostEstimate(flops=1 << 18, bytes_accessed=moved, transcendentals=0),
    )


def copies_kernel(plan, order, partial, *rest):
    outs, sems = rest[:-1], rest[-1]
    started = []
    for number, (output, entry, which, part, rows) in enumerate(plan):
        half = partial.shape[1] // 2
        source = partial.at[
            order[which], pl.ds(part * half, half), pl.ds(rows[0], rows[1] - rows[0])
        ]
        target = outs[output] if entry is None else outs[output].at[entry]
        copy = pltpu.make_async_copy(source, target, sems.at[number])
        copy.start()
        started.append(copy)
    for copy in started:
        copy.wait()


def add_kernel(top_own, low_own, top_in, low_in, top_out, low_out):
    top_out[...] = top_own[...] + top_in[1]
    low_out[...] = low_own[...] + low_in[1]


def join_kernel(
    top_own, low_own, top_near, low_near, top_far, low_far, before, out
):
    half, _ = top_far.shape[:2]
    done = before.shape[1]
    out[:, 0:done] = before[...]
    out[0:half, done:] = top_own[...] + top_near[0] + top_far[...]
    out[half:, done:] = low_own[...] + low_near[0] + low_far[...]


def sum_kernel(top_own, low_own, top_near, low_near, top_far, low_far, out):
    half = top_far.shape[0]
    out[0:half] = top_own[...] + top_near[0] + top_far[...]
    out[half:] = low_own[...] + low_near[0] + low_far[...]


def pair_rows(t):
    return pl.ds(pl.multiple_of(t * 2, 2), 2)


def mark_kernel(slots, target, mask, count):
    mask[...] = jnp.zeros_like(mask)
    ones = jnp.ones((2, mask.shape[1]), f32)

    def source(s, carry):
        for j in range(slots):
            mask[pair_rows(target[s * slots + j])] = ones
        return carry

    lax.fori_loop(0, target.shape[0] // slots, source, 0)
    count[...] = jnp.sum(mask[0 : mask.shape[0] - 8], axis=0, keepdims=True)


def scatter_kernel(slots, target, rows, count, dense, message):
    dense[...] = jnp.zeros_like(dense)

    def source(s, carry):
        base = s * slots
        at = [target[base + j] for j in range(slots)]
        new = [dense[pair_rows(t)] + rows[pair_rows(base + j)] for j, t in enumerate(at)]
        for t, v in zip(at, new):
            dense[pair_rows(t)] = v
        return carry

    lax.fori_loop(0, target.shape[0] // slots, source, 0)
    values = dense[0 : dense.shape[0] - 8]
    square = jnp.sum(jnp.sum(values * values, axis=0, keepdims=True), axis=1, keepdims=True)
    touched = jnp.sum(count[...], axis=1, keepdims=True)
    lane = lax.broadcasted_iota(jnp.int32, (1, 128), 1)
    row = jnp.where(lane == 0, square, jnp.where(lane == 1, touched, 0.0))
    message[...] = jnp.broadcast_to(row, message.shape)


def update_kernel(messages, dense, mask, p_in, m_in, v_in, *rest):
    outs, held, made, sems, done = rest[:3], rest[3:6], rest[6:9], rest[9], rest[10]
    size = p_in.shape[0] // STEPS
    spans = [pl.ds(step * size, size) for step in range(STEPS)]
    loads = []
    for step, at in enumerate(spans):
        for k, source in enumerate((p_in, m_in, v_in)):
            copy = pltpu.make_async_copy(source.at[at], held[k].at[at], sems.at[k, step])
            copy.start()
            loads.append(copy)
    total = jnp.sum(messages[...], axis=0, keepdims=True)
    square, touched = total[0:1, 0:1], total[0:1, 1:2]
    rms = jnp.sqrt(square / touched + 1e-06)
    scale = jnp.minimum(jnp.float32(1.0), 0.5 / rms)
    first, second = 0.1 * scale, 0.01 * scale * scale
    copies = []
    for step, at in enumerate(spans):
        for copy in loads[3 * step : 3 * step + 3]:
            copy.wait()
        grad, live = dense[at], mask[at]
        new_m = held[1][at] * (1.0 - 0.1 * live) + first * grad
        new_v = held[2][at] * (1.0 - 0.01 * live) + second * grad * grad
        root = jnp.sqrt(new_v * (1.0 / (1.0 - 0.99**8))) + 1e-08
        made[0][at] = held[0][at] - (live * (0.01 / (1.0 - 0.9**8))) * new_m / root
        made[1][at] = new_m
        made[2][at] = new_v
        for k in range(3):
            copy = pltpu.make_async_copy(made[k].at[at], outs[k].at[at], done.at[k, step])
            copy.start()
            copies.append(copy)
    for copy in copies:
        copy.wait()


def in_hbm(array):
    return pltpu.with_memory_space_constraint(array, pltpu.HBM)


def shape(*dims):
    return jax.ShapeDtypeStruct(dims, f32)


def step(grad_parts, block_ids, block_counts, params, first_moment, second_moment):
    member = lax.axis_index("grp")
    _, _, groups, owners, slots, features, lanes = grad_parts.shape
    blocks = params.shape[0] * params.shape[1]
    devices = groups * owners
    half = owners // 2
    partial = in_hbm(grad_parts.reshape(groups, owners, slots * features, lanes))

    ids = lax.dynamic_index_in_dim(block_ids[0], member, 0, keepdims=False)
    counts = lax.dynamic_index_in_dim(block_counts[0], member, 0, keepdims=False)
    valid = jnp.arange(slots, dtype=jnp.int32)[None, :] < counts[:, None]
    named = jnp.where(valid, ids, blocks).astype(f32)
    named = jnp.pad(named, ((0, 0), (0, lanes - slots))).reshape(owners, 1, lanes)
    named = lax.all_to_all(named, OWN, split_axis=0, concat_axis=0, tiled=True)
    target = named.reshape(owners, lanes)[:, :slots].astype(jnp.int32).reshape(-1)

    flip, mirror = member ^ 1, 3 - member
    order = jnp.stack([flip, mirror, mirror ^ 1, member])
    flips = [(k, k ^ 1) for k in range(groups)]
    mirrors = [(k, 3 - k) for k in range(groups)]

    def copied(outs, plan):
        return kernel_call(
            functools.partial(copies_kernel, plan),
            outs,
            [SMEM, ANY],
            (VMEM,) * len(outs),
            [pltpu.SemaphoreType.DMA((len(plan),))],
            moved=2 * len(plan) << 18,
        )(order, partial)

    spans = [(sum(CHUNKS[:k]) * features, sum(CHUNKS[: k + 1]) * features) for k in (0, 1)]
    arrived = []
    for span in spans:
        size = span[1] - span[0]
        both = shape(2, half, size, lanes)
        plan = ((0, 0, 0, 0, span), (1, 0, 1, 1, span), (0, 1, 2, 0, span), (1, 1, 2, 1, span))
        top, low = copied((both, both), plan)
        top_in = lax.ppermute(top, "grp", flips)
        low_in = lax.ppermute(low, "grp", mirrors)
        arrived.append([top_in, low_in])
    outs, plan = [], []
    for span in spans:
        for which, part in ((1, 0), (0, 1), (3, 0), (3, 1)):
            plan.append((len(outs), None, which, part, span))
            outs.append(shape(half, span[1] - span[0], lanes))
    kept = copied(tuple(outs), tuple(plan))
    share = None
    for k, span in enumerate(spans):
        size = span[1] - span[0]
        piece = shape(half, size, lanes)
        top_in, low_in = arrived[k]
        far_top, far_low, own_top, own_low = kept[4 * k : 4 * k + 4]
        top, low = kernel_call(add_kernel, (piece, piece), [VMEM] * 4, (VMEM, VMEM))(
            far_top, far_low, top_in, low_in
        )
        top_far = lax.ppermute(top, "grp", mirrors)
        low_far = lax.ppermute(low, "grp", flips)
        pieces = (own_top, own_low, top_in, low_in, top_far, low_far)
        if share is None:
            share = kernel_call(sum_kernel, shape(owners, size, lanes), [VMEM] * 6, VMEM)(*pieces)
        else:
            share = kernel_call(
                join_kernel, shape(owners, span[1], lanes), [VMEM] * 7, VMEM
            )(*pieces, share)
    share = lax.all_to_all(share, OWN, split_axis=0, concat_axis=0, tiled=True)
    share = share.reshape(owners * slots * features, lanes)

    rows = blocks * features
    table = shape(rows + 8, lanes)
    mask, count = kernel_call(
        functools.partial(mark_kernel, slots), (table, shape(1, lanes)), [SMEM], (VMEM, VMEM)
    )(target)
    dense, message = kernel_call(
        functools.partial(scatter_kernel, slots),
        (table, shape(devices, lanes)),
        [SMEM, VMEM, VMEM],
        (VMEM, VMEM),
    )(target, share, count)
    messages = lax.all_to_all(
        message.reshape(devices, 1, lanes), GRP_OWN, split_axis=0, concat_axis=0, tiled=True
    ).reshape(devices, lanes)
    flat = shape(rows, lanes)
    state = [in_hbm(a.reshape(rows, lanes)) for a in (params, first_moment, second_moment)]
    outs = kernel_call(
        update_kernel,
        (flat,) * 3,
        [VMEM] * 3 + [ANY] * 3,
        (ANY,) * 3,
        [pltpu.VMEM((rows, lanes), f32)] * 6 + [pltpu.SemaphoreType.DMA((3, STEPS))] * 2,
    )(messages, dense, mask, *state)
    return tuple(out.reshape(params.shape) for out in outs)


def solution(mesh):
    split = Mesh(
        mesh.devices.reshape(mesh.shape["grp"], 4, 8, 2), ("grp", "own_0", "own_1", "own_2")
    )
    in_specs = (
        P("grp", OWN, None, None, None, None, None),
        P(OWN, None, None, None),
        P(OWN, None, None),
        P(None, GRP_OWN, None, None),
        P(None, GRP_OWN, None, None),
        P(None, GRP_OWN, None, None),
    )
    out_specs = (
        P(None, GRP_OWN, None, None),
        P(None, GRP_OWN, None, None),
        P(None, GRP_OWN, None, None),
    )
    return jax.shard_map(step, mesh=split, in_specs=in_specs, out_specs=out_specs, check_vma=False)
```

time: 169 us -> 121 us (0.72)
  blocking collectives: 60.7 us -> 21.1 us
  Pallas kernels: 0 us -> 20.1 us
  other arithmetic: 19.8 us -> 0.79 us
  starting transfers between devices: 10.8 us -> 29.2 us
  between operations: 15.4 us -> 0.76 us
  waiting for transfers between devices: 50 us -> 42.4 us
  local copies, waits for them, and re-layouts: 12 us -> 5.75 us
    psum x4 -> x0, blocking collectives: 38.5 us -> none  [over_axes(): value = lax.psum(value, axis)]
    reduce_scatter x1 -> x0, waiting for transfers between devices: 30.2 us -> none  [shards(): lax.psum_scatter(partial_value, 'grp', scatter_dimension=0, tiled=True)[0]]
    pallas_call x0 -> x10, Pallas kernels: none -> 20.1 us  [the longest x3 7.58 us: copied(): kernel_call(functools.partial(copies_kernel, plan), outs, [SMEM, ANY], (V...]
    scatter-add x2 -> x0, other arithmetic: 14.6 us -> none  [the longest x1 7.62 us: shards(): jax.ops.segment_sum(valid.reshape(-1).astype(jnp.int32), target, num_segm...]
    all_to_all x1 -> x2, waiting for transfers between devices: 19.8 us -> 32.3 us  [the longest x1 26.2 us: step(): share = lax.all_to_all(share, OWN, split_axis=0, concat_axis=0, tiled=True)]
    ppermute x0 -> x8, waiting for transfers between devices: none -> 10.1 us  [the longest x2 5.86 us: step(): low_in = lax.ppermute(low, 'grp', mirrors)]
    ppermute x0 -> x8, starting transfers between devices: none -> 9.25 us  [the longest x2 4.27 us: step(): top_far = lax.ppermute(top, 'grp', mirrors)]
    all_to_all x1 -> x2, starting transfers between devices: 10.8 us -> 19.9 us  [the longest x1 15.1 us: step(): named = lax.all_to_all(named, OWN, split_axis=0, concat_axis=0, tiled=True)]
  transfers between devices with their start and end apart: 2 -> 10, of which waited for: 2 -> 6; matrix products, arithmetic and copies ran while one was open for 6% -> 1% of each run, Pallas kernels for 0% -> 9%
where the time goes in v1:
time: 121 us; the launch traced here: 120 us
  waiting for transfers between devices  42.4 us (35%)
  starting transfers between devices  29.2 us (24%)
  blocking collectives  21.1 us (17%)
  Pallas kernels  20.1 us (17%)
  local copies, waits for them, and re-layouts  5.75 us (5%)
    all_to_all x1, waiting for transfers between devices, step(): share = lax.all_to_all(share, OWN, split_axis=0, concat_axis=0, tiled=True)  26.2 us
    all_to_all x1, blocking collectives, step(): lax.all_to_all(message.reshape(devices, 1, lanes), GRP_OWN, split_axis=0,...  21.1 us
    all_to_all x1, starting transfers between devices, step(): named = lax.all_to_all(named, OWN, split_axis=0, concat_axis=0, tiled=True)  15.1 us
    pallas_call x3, Pallas kernels, copied(): kernel_call(functools.partial(copies_kernel, plan), outs, [SMEM, ANY], (V...  7.58 us
    all_to_all x1, waiting for transfers between devices, step(): named = lax.all_to_all(named, OWN, split_axis=0, concat_axis=0, tiled=True)  6.11 us
    ppermute x2, waiting for transfers between devices, step(): low_in = lax.ppermute(low, 'grp', mirrors)  5.86 us
    unnamed x14, local copies, waits for them, and re-layouts  4.95 us
    all_to_all x1, starting transfers between devices, step(): share = lax.all_to_all(share, OWN, split_axis=0, concat_axis=0, tiled=True)  4.75 us
  transfers between devices with their start and end apart: 10, of which 6 were waited for; matrix products, arithmetic and copies ran while one was open for 1% of the time, Pallas kernels for 9%

profile of v1, /device:TPU:1, one launch (start us, length us, event | category | flops | bytes accessed | tf_op | source)
XLA Modules:
  0.0 120.1 jit_solution(6260252956964865902)
XLA Ops:
  0.6 0.0 copy-start
  0.7 0.1 pad_add_fusion.order
  0.7 2.7 %shard_map.88 = (f32[2,32,16,128]{3,2,1,0:T(8,128)}, f32[2,32,16,128]{3,2,1,0:T(8,128)}) custom-call(s32[4]{0:T(128)S(1)} %pad_add_fusion.order, f32[4,64,32,128]{3,2,1,0:T(8,128)} %bitcast.28), custom_call_target="tpu_custom_call" | custom-call | flops 262144 | bytes 2097152 | tf_op jit(solution)/shard_map/pallas_call | solution.py:173
  3.5 2.1 %collective-permute-start.4 = (f32[2,32,16,128]{3,2,1,0:T(8,128)}, f32[2,32,16,128]{3,2,1,0:T(8,128)S(1)}, u32[]{:S(2)}, u32[]{:S(2)}) collective-permute-start(f32[2,32,16,128]{3,2,1,0:T(8,128)} %get-tuple-element.36), channel_id=1, source_target_pairs={{0,64},{64,0},{128,192},{192,128},{1,65},{65,1},{129,193},{193,129... | collective-permute-start | bytes 1572872 | tf_op jit(solution)/shard_map/ppermute | solution.py:189
  5.6 1.8 %collective-permute-start.5 = (f32[2,32,16,128]{3,2,1,0:T(8,128)}, f32[2,32,16,128]{3,2,1,0:T(8,128)S(1)}, u32[]{:S(2)}, u32[]{:S(2)}) collective-permute-start(f32[2,32,16,128]{3,2,1,0:T(8,128)} %get-tuple-element.37), channel_id=1, source_target_pairs={{0,192},{64,128},{128,64},{192,0},{1,193},{65,129},{129,65},{193,1... | collective-permute-start | bytes 1572872 | tf_op jit(solution)/shard_map/ppermute | solution.py:190
  7.4 2.7 %shard_map.86 = (f32[2,32,16,128]{3,2,1,0:T(8,128)}, f32[2,32,16,128]{3,2,1,0:T(8,128)}) custom-call(s32[4]{0:T(128)S(1)} %pad_add_fusion.order, f32[4,64,32,128]{3,2,1,0:T(8,128)} %bitcast.29), custom_call_target="tpu_custom_call" | custom-call | flops 262144 | bytes 2097152 | tf_op jit(solution)/shard_map/pallas_call | solution.py:173
  10.1 0.4 collective-permute-start
  10.5 0.6 collective-permute-start.1
  11.2 2.1 %shard_map.85 = (f32[32,16,128]{2,1,0:T(8,128)S(1)}, f32[32,16,128]{2,1,0:T(8,128)S(1)}, f32[32,16,128]{2,1,0:T(8,128)S(1)}, f32[32,16,128]{2,1,0:T(8,128)S(1)},...) custom-call(s32[4]{0:T(128)S(1)} %pad_add_fusion.order, ...), custom_call_target="tpu_custom_call" | custom-call | flops 262144 | bytes 4194304 | tf_op jit(solution)/shard_map/pallas_call | solution.py:173
  13.3 0.0 copy-start.1
  13.3 0.7 copy-done.1
  14.0 0.0 copy-start.3
  14.0 0.7 copy-done.3
  14.7 0.0 copy-start.5
  14.7 0.7 copy-done.5
  15.4 0.0 copy-done
  15.4 0.9 collective-permute-done.4.top_in.top_near
  16.3 2.9 %collective-permute-done.5.low_in.low_near = f32[2,32,16,128]{3,2,1,0:T(8,128)S(1)} collective-permute-done((f32[2,32,16,128]{3,2,1,0:T(8,128)}, f32[2,32,16,128]{3,2,1,0:T(8,128)S(1)}, u32[]{:S(2)}, u32[]{:S(2)}) %collective-permute-start.5) | collective-permute-done | bytes 524320 | tf_op jit(solution)/shard_map/ppermute | solution.py:190
  19.2 0.0 copy-start.4
  19.2 0.9 copy-done.4
  20.2 0.0 copy-start.6
  20.2 0.9 copy-done.6
  21.1 0.9 shard_map.89
  22.0 2.1 %collective-permute-start.6 = (f32[32,16,128]{2,1,0:T(8,128)}, f32[32,16,128]{2,1,0:T(8,128)}, u32[]{:S(2)}, u32[]{:S(2)}) collective-permute-start(f32[32,16,128]{2,1,0:T(8,128)} %get-tuple-element.40), channel_id=1, source_target_pairs={{0,192},{64,128},{128,64},{192,0},{1,193},{65,129},{129,65},{193,1... | collective-permute-start | bytes 786440 | tf_op jit(solution)/shard_map/ppermute | solution.py:207
  24.1 0.0 collective-permute-start.7
  24.1 3.4 %collective-permute-done.top_in.top_near = f32[2,32,16,128]{3,2,1,0:T(8,128)S(1)} collective-permute-done((f32[2,32,16,128]{3,2,1,0:T(8,128)}, f32[2,32,16,128]{3,2,1,0:T(8,128)S(1)}, u32[]{:S(2)}, u32[]{:S(2)}) %collective-permute-start) | collective-permute-done | bytes 524320 | tf_op jit(solution)/shard_map/ppermute | solution.py:189
  27.5 2.9 %collective-permute-done.1.low_in.low_near = f32[2,32,16,128]{3,2,1,0:T(8,128)S(1)} collective-permute-done((f32[2,32,16,128]{3,2,1,0:T(8,128)}, f32[2,32,16,128]{3,2,1,0:T(8,128)S(1)}, u32[]{:S(2)}, u32[]{:S(2)}) %collective-permute-start.1) | collective-permute-done | bytes 524320 | tf_op jit(solution)/shard_map/ppermute | solution.py:190
  30.5 0.8 shard_map.87
  31.3 2.1 %collective-permute-start.2 = (f32[32,16,128]{2,1,0:T(8,128)}, f32[32,16,128]{2,1,0:T(8,128)S(1)}, u32[]{:S(2)}, u32[]{:S(2)}) collective-permute-start(f32[32,16,128]{2,1,0:T(8,128)} %get-tuple-element.32), channel_id=1, source_target_pairs={{0,192},{64,128},{128,64},{192,0},{1,193},{65,129},{129,65},{193,1... | collective-permute-start | bytes 786440 | tf_op jit(solution)/shard_map/ppermute | solution.py:207
  33.4 0.0 collective-permute-start.3
  33.4 0.7 fusion
  34.1 0.7 copy.10
  34.9 15.1 %all-to-all-start = ((f32[64,1,128]{2,1,0:T(1,128)}), f32[64,1,128]{2,1,0:T(1,128)S(1)}, u32[]{:S(2)}, u32[]{:S(2)}) async-start(f32[64,1,128]{2,1,0:T(1,128)} %copy.10), calls=%async_computation | async-start | bytes 65536 | tf_op jit(solution)/shard_map/all_to_all | solution.py:164
  50.0 0.0 collective-permute-done.6.top_far
  50.0 0.0 collective-permute-done.7.low_far
  50.0 0.0 copy-start.2
  50.0 0.9 copy-done.2
  51.0 1.1 shard_map.90.before
  52.1 0.0 collective-permute-done.2.top_far
  52.1 0.0 collective-permute-done.3.low_far
  52.1 1.1 shard_map.91
  53.2 6.1 %all-to-all-done = f32[64,1,128]{2,1,0:T(1,128)S(1)} async-done(((f32[64,1,128]{2,1,0:T(1,128)}), f32[64,1,128]{2,1,0:T(1,128)S(1)}, u32[]{:S(2)}, u32[]{:S(2)}) %all-to-all-start) | async-done | bytes 32800 | tf_op jit(solution)/shard_map/all_to_all | solution.py:164
  59.3 4.7 %all-to-all-start.1 = ((f32[64,32,128]{2,1,0:T(8,128)}), f32[64,32,128]{2,1,0:T(8,128)S(1)}, u32[]{:S(2)}, u32[]{:S(2)}) async-start(f32[64,32,128]{2,1,0:T(8,128)} %shard_map.91), calls=%async_computation.1 | async-start | bytes 2097152 | tf_op jit(solution)/shard_map/all_to_all | solution.py:216
  64.1 0.1 reshape.53.target
  64.2 2.3 %shard_map.92 = (f32[2056,128]{1,0:T(8,128)S(1)}, f32[1,128]{1,0:T(1,128)S(1)}) custom-call(s32[1024]{0:T(1024)S(1)} %reshape.53.target), custom_call_target="tpu_custom_call" | custom-call | flops 262144 | bytes 1048576 | tf_op jit(solution)/shard_map/pallas_call | solution.py:221
  66.4 26.2 %all-to-all-done.1 = f32[64,32,128]{2,1,0:T(8,128)S(1)} async-done(((f32[64,32,128]{2,1,0:T(8,128)}), f32[64,32,128]{2,1,0:T(8,128)S(1)}, u32[]{:S(2)}, u32[]{:S(2)}) %all-to-all-start.1) | async-done | bytes 1048608 | tf_op jit(solution)/shard_map/all_to_all | solution.py:216
  92.6 2.9 %shard_map.93 = (f32[2056,128]{1,0:T(8,128)S(1)}, f32[256,128]{1,0:T(8,128)S(1)}) custom-call(s32[1024]{0:T(1024)S(1)} %reshape.53.target, f32[2048,128]{1,0:T(8,128)S(1)} %bitcast.25, f32[1,128]{1,0:T(1,128)S(1)} %get-tuple-element.42.count), custom_call_target="tpu_custom_call" | custom-call | flops 262144 | bytes 1048576 | tf_op jit(solution)/shard_map/pallas_call | solution.py:224
  95.6 21.1 %all_to_all.15 = f32[256,1,128]{2,1,0:T(1,128)S(1)} all-to-all(f32[256,1,128]{2,1,0:T(1,128)S(1)} %bitcast.27), channel_id=1, replica_groups=mesh['grp'=4,'own_0'=4,'own_1'=8,'own_2'=2] {'grp','own_0','own_1','own_2'}, dimensions={0} | all-to-all | bytes 262144 | tf_op jit(solution)/shard_map/all_to_all | solution.py:230
  116.7 3.4 %shard_map.94 = (f32[2048,128]{1,0:T(8,128)}, f32[2048,128]{1,0:T(8,128)}, f32[2048,128]{1,0:T(8,128)}) custom-call(f32[256,128]{1,0:T(8,128)S(1)} %bitcast.26, f32[2056,128]{1,0:T(8,128)S(1)} %get-tuple-element.44.dense, f32[2056,128]{1,0:T(8,128)S(1)} %get-tuple-element.45.mask, f32[2048,128]{1,0:T(8,128)} %bitcast.31, f32[2048,128]{1,0:T(8,128)} %bitcast.32, ...), custom_call_target="tpu_custom_call" | custom-call | flops 262144 | bytes 1048576 | tf_op jit(solution)/shard_map/pallas_call | solution.py:235
  (3 shorter events, 0.0 us)
Async XLA Ops:
  0.6 14.8 %copy-start = (s32[1,4,64]{2,1,0:T(4,128)S(1)}, s32[1,4,64]{2,1,0:T(4,128)}, u32[]{:S(2)}) copy-start(s32[1,4,64]{2,1,0:T(4,128)} %param.8) | copy-start | bytes 3076
  3.5 12.8 %collective-permute-start.4 = (f32[2,32,16,128]{3,2,1,0:T(8,128)}, f32[2,32,16,128]{3,2,1,0:T(8,128)S(1)}, u32[]{:S(2)}, u32[]{:S(2)}) collective-permute-start(f32[2,32,16,128]{3,2,1,0:T(8,128)} %get-tuple-element.36), channel_id=1, source_target_pairs={{0,64},{64,0},{128,192},{192,128},{1,65},{65,1},{129,193},{193,129... | collective-permute-start | bytes 1572872 | tf_op jit(solution)/shard_map/ppermute | solution.py:189
  5.6 13.6 %collective-permute-start.5 = (f32[2,32,16,128]{3,2,1,0:T(8,128)}, f32[2,32,16,128]{3,2,1,0:T(8,128)S(1)}, u32[]{:S(2)}, u32[]{:S(2)}) collective-permute-start(f32[2,32,16,128]{3,2,1,0:T(8,128)} %get-tuple-element.37), channel_id=1, source_target_pairs={{0,192},{64,128},{128,64},{192,0},{1,193},{65,129},{129,65},{193,1... | collective-permute-start | bytes 1572872 | tf_op jit(solution)/shard_map/ppermute | solution.py:190
  10.1 17.4 %collective-permute-start = (f32[2,32,16,128]{3,2,1,0:T(8,128)}, f32[2,32,16,128]{3,2,1,0:T(8,128)S(1)}, u32[]{:S(2)}, u32[]{:S(2)}) collective-permute-start(f32[2,32,16,128]{3,2,1,0:T(8,128)} %get-tuple-element.28), channel_id=1, source_target_pairs={{0,64},{64,0},{128,192},{192,128},{1,65},{65,1},{129,193},{193,129... | collective-permute-start | bytes 1572872 | tf_op jit(solution)/shard_map/ppermute | solution.py:189
  10.5 19.9 %collective-permute-start.1 = (f32[2,32,16,128]{3,2,1,0:T(8,128)}, f32[2,32,16,128]{3,2,1,0:T(8,128)S(1)}, u32[]{:S(2)}, u32[]{:S(2)}) collective-permute-start(f32[2,32,16,128]{3,2,1,0:T(8,128)} %get-tuple-element.29), channel_id=1, source_target_pairs={{0,192},{64,128},{128,64},{192,0},{1,193},{65,129},{129,65},{193,1... | collective-permute-start | bytes 1572872 | tf_op jit(solution)/shard_map/ppermute | solution.py:190
  13.3 0.7 copy-start.1
  14.0 0.7 copy-start.3
  14.7 0.7 copy-start.5
  19.2 1.0 copy-start.4
  20.2 0.9 copy-start.6
  22.0 28.0 %collective-permute-start.6 = (f32[32,16,128]{2,1,0:T(8,128)}, f32[32,16,128]{2,1,0:T(8,128)}, u32[]{:S(2)}, u32[]{:S(2)}) collective-permute-start(f32[32,16,128]{2,1,0:T(8,128)} %get-tuple-element.40), channel_id=1, source_target_pairs={{0,192},{64,128},{128,64},{192,0},{1,193},{65,129},{129,65},{193,1... | collective-permute-start | bytes 786440 | tf_op jit(solution)/shard_map/ppermute | solution.py:207
  24.1 25.9 %collective-permute-start.7 = (f32[32,16,128]{2,1,0:T(8,128)}, f32[32,16,128]{2,1,0:T(8,128)}, u32[]{:S(2)}, u32[]{:S(2)}) collective-permute-start(f32[32,16,128]{2,1,0:T(8,128)} %get-tuple-element.41), channel_id=1, source_target_pairs={{0,64},{64,0},{128,192},{192,128},{1,65},{65,1},{129,193},{193,129... | collective-permute-start | bytes 786440 | tf_op jit(solution)/shard_map/ppermute | solution.py:208
  31.3 20.8 %collective-permute-start.2 = (f32[32,16,128]{2,1,0:T(8,128)}, f32[32,16,128]{2,1,0:T(8,128)S(1)}, u32[]{:S(2)}, u32[]{:S(2)}) collective-permute-start(f32[32,16,128]{2,1,0:T(8,128)} %get-tuple-element.32), channel_id=1, source_target_pairs={{0,192},{64,128},{128,64},{192,0},{1,193},{65,129},{129,65},{193,1... | collective-permute-start | bytes 786440 | tf_op jit(solution)/shard_map/ppermute | solution.py:207
  33.4 18.7 %collective-permute-start.3 = (f32[32,16,128]{2,1,0:T(8,128)}, f32[32,16,128]{2,1,0:T(8,128)S(1)}, u32[]{:S(2)}, u32[]{:S(2)}) collective-permute-start(f32[32,16,128]{2,1,0:T(8,128)} %get-tuple-element.33), channel_id=1, source_target_pairs={{0,64},{64,0},{128,192},{192,128},{1,65},{65,1},{129,193},{193,129... | collective-permute-start | bytes 786440 | tf_op jit(solution)/shard_map/ppermute | solution.py:208
  34.9 24.5 %all-to-all-start = ((f32[64,1,128]{2,1,0:T(1,128)}), f32[64,1,128]{2,1,0:T(1,128)S(1)}, u32[]{:S(2)}, u32[]{:S(2)}) async-start(f32[64,1,128]{2,1,0:T(1,128)} %copy.10), calls=%async_computation | async-start | bytes 65536 | tf_op jit(solution)/shard_map/all_to_all | solution.py:164
  50.0 1.0 copy-start.2
  59.3 33.3 %all-to-all-start.1 = ((f32[64,32,128]{2,1,0:T(8,128)}), f32[64,32,128]{2,1,0:T(8,128)S(1)}, u32[]{:S(2)}, u32[]{:S(2)}) async-start(f32[64,32,128]{2,1,0:T(8,128)} %shard_map.91), calls=%async_computation.1 | async-start | bytes 2097152 | tf_op jit(solution)/shard_map/all_to_all | solution.py:216

commit v2 on v1

--- a/solution.py
+++ b/solution.py
@@ -53,16 +53,6 @@
     low_out[...] = low_own[...] + low_in[1]
 
 
-def join_kernel(
-    top_own, low_own, top_near, low_near, top_far, low_far, before, out
-):
-    half, _ = top_far.shape[:2]
-    done = before.shape[1]
-    out[:, 0:done] = before[...]
-    out[0:half, done:] = top_own[...] + top_near[0] + top_far[...]
-    out[half:, done:] = low_own[...] + low_near[0] + low_far[...]
-
-
 def sum_kernel(top_own, low_own, top_near, low_near, top_far, low_far, out):
     half = top_far.shape[0]
     out[0:half] = top_own[...] + top_near[0] + top_far[...]
@@ -86,18 +76,34 @@
     count[...] = jnp.sum(mask[0 : mask.shape[0] - 8], axis=0, keepdims=True)
 
 
-def scatter_kernel(slots, target, rows, count, dense, message):
-    dense[...] = jnp.zeros_like(dense)
-
-    def source(s, carry):
-        base = s * slots
-        at = [target[base + j] for j in range(slots)]
-        new = [dense[pair_rows(t)] + rows[pair_rows(base + j)] for j, t in enumerate(at)]
-        for t, v in zip(at, new):
-            dense[pair_rows(t)] = v
+def scatter_rows(slots, first, width, target, rows, even, odd):
+    even[...] = jnp.zeros_like(even)
+    odd[...] = jnp.zeros_like(odd)
+
+    def sources(s, carry):
+        picks = []
+        for k, ref in ((0, even), (1, odd)):
+            for j in range(width):
+                picks.append((ref, target[(2 * s + k) * slots + first + j]))
+        new = [
+            ref[pair_rows(t)] + rows[pair_rows(2 * s * width + j)]
+            for j, (ref, t) in enumerate(picks)
+        ]
+        for (ref, t), value in zip(picks, new):
+            ref[pair_rows(t)] = value
         return carry
 
-    lax.fori_loop(0, target.shape[0] // slots, source, 0)
+    lax.fori_loop(0, target.shape[0] // (2 * slots), sources, 0)
+
+
+def first_kernel(slots, width, target, rows, dense, other):
+    scatter_rows(slots, 0, width, target, rows, dense, other)
+    dense[...] += other[...]
+
+
+def last_kernel(slots, first, width, target, rows, before, count, dense, message, other):
+    scatter_rows(slots, first, width, target, rows, dense, other)
+    dense[...] += other[...] + before[...]
     values = dense[0 : dense.shape[0] - 8]
     square = jnp.sum(jnp.sum(values * values, axis=0, keepdims=True), axis=1, keepdims=True)
     touched = jnp.sum(count[...], axis=1, keepdims=True)
@@ -180,53 +186,46 @@
         )(order, partial)
 
     spans = [(sum(CHUNKS[:k]) * features, sum(CHUNKS[: k + 1]) * features) for k in (0, 1)]
-    arrived = []
+    shares = []
     for span in spans:
         size = span[1] - span[0]
-        both = shape(2, half, size, lanes)
+        piece, both = shape(half, size, lanes), shape(2, half, size, lanes)
         plan = ((0, 0, 0, 0, span), (1, 0, 1, 1, span), (0, 1, 2, 0, span), (1, 1, 2, 1, span))
         top, low = copied((both, both), plan)
         top_in = lax.ppermute(top, "grp", flips)
         low_in = lax.ppermute(low, "grp", mirrors)
-        arrived.append([top_in, low_in])
-    outs, plan = [], []
-    for span in spans:
-        for which, part in ((1, 0), (0, 1), (3, 0), (3, 1)):
-            plan.append((len(outs), None, which, part, span))
-            outs.append(shape(half, span[1] - span[0], lanes))
-    kept = copied(tuple(outs), tuple(plan))
-    share = None
-    for k, span in enumerate(spans):
-        size = span[1] - span[0]
-        piece = shape(half, size, lanes)
-        top_in, low_in = arrived[k]
-        far_top, far_low, own_top, own_low = kept[4 * k : 4 * k + 4]
+        plan = tuple(
+            (n, None, which, part, span)
+            for n, (which, part) in enumerate(((1, 0), (0, 1), (3, 0), (3, 1)))
+        )
+        far_top, far_low, own_top, own_low = copied((piece,) * 4, plan)
         top, low = kernel_call(add_kernel, (piece, piece), [VMEM] * 4, (VMEM, VMEM))(
             far_top, far_low, top_in, low_in
         )
         top_far = lax.ppermute(top, "grp", mirrors)
         low_far = lax.ppermute(low, "grp", flips)
-        pieces = (own_top, own_low, top_in, low_in, top_far, low_far)
-        if share is None:
-            share = kernel_call(sum_kernel, shape(owners, size, lanes), [VMEM] * 6, VMEM)(*pieces)
-        else:
-            share = kernel_call(
-                join_kernel, shape(owners, span[1], lanes), [VMEM] * 7, VMEM
-            )(*pieces, share)
-    share = lax.all_to_all(share, OWN, split_axis=0, concat_axis=0, tiled=True)
-    share = share.reshape(owners * slots * features, lanes)
+        share = kernel_call(sum_kernel, shape(owners, size, lanes), [VMEM] * 6, VMEM)(
+            own_top, own_low, top_in, low_in, top_far, low_far
+        )
+        share = lax.all_to_all(share, OWN, split_axis=0, concat_axis=0, tiled=True)
+        shares.append(share.reshape(owners * size, lanes))
 
     rows = blocks * features
     table = shape(rows + 8, lanes)
     mask, count = kernel_call(
         functools.partial(mark_kernel, slots), (table, shape(1, lanes)), [SMEM], (VMEM, VMEM)
     )(target)
+    spare = [pltpu.VMEM(table.shape, f32)]
+    before = kernel_call(
+        functools.partial(first_kernel, slots, CHUNKS[0]), table, [SMEM, VMEM], VMEM, spare
+    )(target, shares[0])
     dense, message = kernel_call(
-        functools.partial(scatter_kernel, slots),
+        functools.partial(last_kernel, slots, CHUNKS[0], CHUNKS[1]),
         (table, shape(devices, lanes)),
-        [SMEM, VMEM, VMEM],
+        [SMEM] + [VMEM] * 3,
         (VMEM, VMEM),
-    )(target, share, count)
+        spare,
+    )(target, shares[1], before, count)
     messages = lax.all_to_all(
         message.reshape(devices, 1, lanes), GRP_OWN, split_axis=0, concat_axis=0, tiled=True
     ).reshape(devices, lanes)

time: 121 us -> 132 us (1.091)
  starting transfers between devices: 29.2 us -> 41.1 us
  waiting for transfers between devices: 42.4 us -> 49.2 us
  local copies, waits for them, and re-layouts: 5.75 us -> 0.8 us
  Pallas kernels: 20.1 us -> 18.2 us
    all_to_all x1 -> x2, waiting for transfers between devices: 26.2 us -> 13.4 us  [step(): share = lax.all_to_all(share, OWN, split_axis=0, concat_axis=0, tiled=True)]
    all_to_all x1 -> x2, starting transfers between devices: 4.75 us -> 17.5 us  [step(): share = lax.all_to_all(share, OWN, split_axis=0, concat_axis=0, tiled=True)]
    ppermute x2, waiting for transfers between devices: 4.25 us -> 15.9 us  [step(): top_in = lax.ppermute(top, 'grp', flips)]
    ppermute x2, waiting for transfers between devices: 0.01 us -> 6.51 us  [step(): top_far = lax.ppermute(top, 'grp', mirrors)]
    unnamed x14 -> x2, local copies, waits for them, and re-layouts: 4.95 us -> 0.01 us
    all_to_all x1, waiting for transfers between devices: 6.11 us -> 8.35 us  [step(): named = lax.all_to_all(named, OWN, split_axis=0, concat_axis=0, tiled=True)]
    pallas_call x2, Pallas kernels: 1.71 us -> 0.11 us  [step(): kernel_call(add_kernel, (piece, piece), [VMEM] * 4, (VMEM, VMEM))]
    ppermute x2, starting transfers between devices: 2.52 us -> 3.95 us  [step(): top_in = lax.ppermute(top, 'grp', flips)]
  transfers between devices with their start and end apart: 10 -> 11, of which waited for: 6 -> 7; matrix products, arithmetic and copies ran while one was open for 1% -> 1% of each run, Pallas kernels for 9% -> 8%
where the time goes in v2:
time: 132 us; the launch traced here: 131 us
  waiting for transfers between devices  49.2 us (37%)
  starting transfers between devices  41.1 us (31%)
  blocking collectives  20.3 us (15%)
  Pallas kernels  18.2 us (14%)
    all_to_all x1, blocking collectives, step(): lax.all_to_all(message.reshape(devices, 1, lanes), GRP_OWN, split_axis=0,...  20.3 us
    all_to_all x2, starting transfers between devices, step(): share = lax.all_to_all(share, OWN, split_axis=0, concat_axis=0, tiled=True)  17.5 us
    ppermute x2, waiting for transfers between devices, step(): top_in = lax.ppermute(top, 'grp', flips)  15.9 us
    all_to_all x1, starting transfers between devices, step(): named = lax.all_to_all(named, OWN, split_axis=0, concat_axis=0, tiled=True)  13.7 us
    all_to_all x2, waiting for transfers between devices, step(): share = lax.all_to_all(share, OWN, split_axis=0, concat_axis=0, tiled=True)  13.4 us
    all_to_all x1, waiting for transfers between devices, step(): named = lax.all_to_all(named, OWN, split_axis=0, concat_axis=0, tiled=True)  8.35 us
    pallas_call x4, Pallas kernels, copied(): kernel_call(functools.partial(copies_kernel, plan), outs, [SMEM, ANY], (V...  7.06 us
    ppermute x2, waiting for transfers between devices, step(): top_far = lax.ppermute(top, 'grp', mirrors)  6.51 us
  transfers between devices with their start and end apart: 11, of which 7 were waited for; matrix products, arithmetic and copies ran while one was open for 1% of the time, Pallas kernels for 8%

profile of v2, /device:TPU:1, one launch (start us, length us, event | category | flops | bytes accessed | tf_op | source)
XLA Modules:
  0.0 131.1 jit_solution(14076655256569873690)
XLA Ops:
  0.6 0.0 copy-start
  0.7 0.1 pad_add_fusion.order
  0.7 1.8 %shard_map.90 = (f32[2,32,16,128]{3,2,1,0:T(8,128)S(1)}, f32[2,32,16,128]{3,2,1,0:T(8,128)S(1)}) custom-call(s32[4]{0:T(128)S(1)} %pad_add_fusion.order, f32[4,64,32,128]{3,2,1,0:T(8,128)} %bitcast.30), custom_call_target="tpu_custom_call" | custom-call | flops 262144 | bytes 2097152 | tf_op jit(solution)/shard_map/pallas_call | solution.py:179
  2.5 2.1 %collective-permute-start.4 = (f32[2,32,16,128]{3,2,1,0:T(8,128)S(1)}, f32[2,32,16,128]{3,2,1,0:T(8,128)S(1)}, u32[]{:S(2)}, u32[]{:S(2)}) collective-permute-start(f32[2,32,16,128]{3,2,1,0:T(8,128)S(1)} %get-tuple-element.36), channel_id=1, source_target_pairs={{0,64},{64,0},{128,192},{192,128},{1,65},{65,1},{129,193},{193,129... | collective-permute-start | bytes 1572872 | tf_op jit(solution)/shard_map/ppermute | solution.py:195
  4.6 1.8 %collective-permute-start.5 = (f32[2,32,16,128]{3,2,1,0:T(8,128)S(1)}, f32[2,32,16,128]{3,2,1,0:T(8,128)S(1)}, u32[]{:S(2)}, u32[]{:S(2)}) collective-permute-start(f32[2,32,16,128]{3,2,1,0:T(8,128)S(1)} %get-tuple-element.37), channel_id=1, source_target_pairs={{0,192},{64,128},{128,64},{192,0},{1,193},{65,129},{129,65},{193,1... | collective-permute-start | bytes 1572872 | tf_op jit(solution)/shard_map/ppermute | solution.py:196
  6.4 1.8 %shard_map.89 = (f32[32,16,128]{2,1,0:T(8,128)S(1)}, f32[32,16,128]{2,1,0:T(8,128)S(1)}, f32[32,16,128]{2,1,0:T(8,128)S(1)}, f32[32,16,128]{2,1,0:T(8,128)S(1)}) custom-call(s32[4]{0:T(128)S(1)} %pad_add_fusion.order, f32[4,64,32,128]{3,2,1,0:T(8,128)} %bitcast.31), custom_call_target="tpu_custom_call" | custom-call | flops 262144 | bytes 2097152 | tf_op jit(solution)/shard_map/pallas_call | solution.py:179
  8.2 0.0 copy-done
  8.2 6.8 %collective-permute-done.4.top_in.top_near = f32[2,32,16,128]{3,2,1,0:T(8,128)S(1)} collective-permute-done((f32[2,32,16,128]{3,2,1,0:T(8,128)S(1)}, f32[2,32,16,128]{3,2,1,0:T(8,128)S(1)}, u32[]{:S(2)}, u32[]{:S(2)}) %collective-permute-start.4) | collective-permute-done | bytes 524320 | tf_op jit(solution)/shard_map/ppermute | solution.py:195
  15.0 3.0 %collective-permute-done.5.low_in.low_near = f32[2,32,16,128]{3,2,1,0:T(8,128)S(1)} collective-permute-done((f32[2,32,16,128]{3,2,1,0:T(8,128)S(1)}, f32[2,32,16,128]{3,2,1,0:T(8,128)S(1)}, u32[]{:S(2)}, u32[]{:S(2)}) %collective-permute-start.5) | collective-permute-done | bytes 524320 | tf_op jit(solution)/shard_map/ppermute | solution.py:196
  18.0 0.1 shard_map.91
  18.1 2.2 %collective-permute-start.6 = (f32[32,16,128]{2,1,0:T(8,128)S(1)}, f32[32,16,128]{2,1,0:T(8,128)S(1)}, u32[]{:S(2)}, u32[]{:S(2)}) collective-permute-start(f32[32,16,128]{2,1,0:T(8,128)S(1)} %get-tuple-element.40), channel_id=1, source_target_pairs={{0,192},{64,128},{128,64},{192,0},{1,193},{65,129},{129,65},{193,1... | collective-permute-start | bytes 786440 | tf_op jit(solution)/shard_map/ppermute | solution.py:205
  20.3 0.0 collective-permute-start.7
  20.3 0.7 fusion
  21.0 0.7 copy.10
  21.7 13.7 %all-to-all-start = ((f32[64,1,128]{2,1,0:T(1,128)}), f32[64,1,128]{2,1,0:T(1,128)S(1)}, u32[]{:S(2)}, u32[]{:S(2)}) async-start(f32[64,1,128]{2,1,0:T(1,128)} %copy.10), calls=%async_computation | async-start | bytes 65536 | tf_op jit(solution)/shard_map/all_to_all | solution.py:170
  35.5 0.0 collective-permute-done.6.top_far
  35.5 0.0 collective-permute-done.7.low_far
  35.5 0.9 shard_map.92
  36.4 8.3 %all-to-all-done = f32[64,1,128]{2,1,0:T(1,128)S(1)} async-done(((f32[64,1,128]{2,1,0:T(1,128)}), f32[64,1,128]{2,1,0:T(1,128)S(1)}, u32[]{:S(2)}, u32[]{:S(2)}) %all-to-all-start) | async-done | bytes 32800 | tf_op jit(solution)/shard_map/all_to_all | solution.py:170
  44.7 4.7 %all-to-all-start.2 = ((f32[64,16,128]{2,1,0:T(8,128)}), f32[64,16,128]{2,1,0:T(8,128)S(1)}, u32[]{:S(2)}, u32[]{:S(2)}) async-start(f32[64,16,128]{2,1,0:T(8,128)} %shard_map.92), calls=%async_computation.2 | async-start | bytes 1048576 | tf_op jit(solution)/shard_map/all_to_all | solution.py:210
  49.5 1.8 %shard_map.86 = (f32[2,32,16,128]{3,2,1,0:T(8,128)S(1)}, f32[2,32,16,128]{3,2,1,0:T(8,128)S(1)}) custom-call(s32[4]{0:T(128)S(1)} %pad_add_fusion.order, f32[4,64,32,128]{3,2,1,0:T(8,128)} %bitcast.32), custom_call_target="tpu_custom_call" | custom-call | flops 262144 | bytes 2097152 | tf_op jit(solution)/shard_map/pallas_call | solution.py:179
  51.2 1.8 %collective-permute-start = (f32[2,32,16,128]{3,2,1,0:T(8,128)S(1)}, f32[2,32,16,128]{3,2,1,0:T(8,128)S(1)}, u32[]{:S(2)}, u32[]{:S(2)}) collective-permute-start(f32[2,32,16,128]{3,2,1,0:T(8,128)S(1)} %get-tuple-element.28), channel_id=1, source_target_pairs={{0,64},{64,0},{128,192},{192,128},{1,65},{65,1},{129,193},{193,129... | collective-permute-start | bytes 1572872 | tf_op jit(solution)/shard_map/ppermute | solution.py:195
  53.1 0.9 collective-permute-start.1
  53.9 1.8 %shard_map.85 = (f32[32,16,128]{2,1,0:T(8,128)S(1)}, f32[32,16,128]{2,1,0:T(8,128)S(1)}, f32[32,16,128]{2,1,0:T(8,128)S(1)}, f32[32,16,128]{2,1,0:T(8,128)S(1)}) custom-call(s32[4]{0:T(128)S(1)} %pad_add_fusion.order, f32[4,64,32,128]{3,2,1,0:T(8,128)} %bitcast.33), custom_call_target="tpu_custom_call" | custom-call | flops 262144 | bytes 2097152 | tf_op jit(solution)/shard_map/pallas_call | solution.py:179
  55.7 9.1 %collective-permute-done.top_in.top_near = f32[2,32,16,128]{3,2,1,0:T(8,128)S(1)} collective-permute-done((f32[2,32,16,128]{3,2,1,0:T(8,128)S(1)}, f32[2,32,16,128]{3,2,1,0:T(8,128)S(1)}, u32[]{:S(2)}, u32[]{:S(2)}) %collective-permute-start) | collective-permute-done | bytes 524320 | tf_op jit(solution)/shard_map/ppermute | solution.py:195
  64.8 2.1 %collective-permute-done.1.low_in.low_near = f32[2,32,16,128]{3,2,1,0:T(8,128)S(1)} collective-permute-done((f32[2,32,16,128]{3,2,1,0:T(8,128)S(1)}, f32[2,32,16,128]{3,2,1,0:T(8,128)S(1)}, u32[]{:S(2)}, u32[]{:S(2)}) %collective-permute-start.1) | collective-permute-done | bytes 524320 | tf_op jit(solution)/shard_map/ppermute | solution.py:196
  66.9 0.1 shard_map.87
  67.0 0.9 collective-permute-start.2
  67.9 0.0 collective-permute-start.3
  67.9 6.5 %collective-permute-done.2.top_far = f32[32,16,128]{2,1,0:T(8,128)S(1)} collective-permute-done((f32[32,16,128]{2,1,0:T(8,128)S(1)}, f32[32,16,128]{2,1,0:T(8,128)S(1)}, u32[]{:S(2)}, u32[]{:S(2)}) %collective-permute-start.2) | collective-permute-done | bytes 262176 | tf_op jit(solution)/shard_map/ppermute | solution.py:205
  74.4 0.0 collective-permute-done.3.low_far
  74.4 0.9 shard_map.88
  75.3 0.0 all-to-all-done.2
  75.3 12.8 %all-to-all-start.1 = ((f32[64,16,128]{2,1,0:T(8,128)}), f32[64,16,128]{2,1,0:T(8,128)S(1)}, u32[]{:S(2)}, u32[]{:S(2)}) async-start(f32[64,16,128]{2,1,0:T(8,128)} %shard_map.88), calls=%async_computation.1 | async-start | bytes 1048576 | tf_op jit(solution)/shard_map/all_to_all | solution.py:210
  88.1 0.1 reshape.56.target
  88.2 2.3 %shard_map.94 = (f32[2056,128]{1,0:T(8,128)S(1)}, f32[1,128]{1,0:T(1,128)S(1)}) custom-call(s32[1024]{0:T(1024)S(1)} %reshape.56.target), custom_call_target="tpu_custom_call" | custom-call | flops 262144 | bytes 1048576 | tf_op jit(solution)/shard_map/pallas_call | solution.py:215
  90.5 1.6 %shard_map.93.before = f32[2056,128]{1,0:T(8,128)S(1)} custom-call(s32[1024]{0:T(1024)S(1)} %reshape.56.target, f32[1024,128]{1,0:T(8,128)S(1)} %bitcast.26), custom_call_target="tpu_custom_call" | custom-call | flops 262144 | bytes 1048576 | tf_op jit(solution)/shard_map/pallas_call | solution.py:219
  92.0 13.4 %all-to-all-done.1 = f32[64,16,128]{2,1,0:T(8,128)S(1)} async-done(((f32[64,16,128]{2,1,0:T(8,128)}), f32[64,16,128]{2,1,0:T(8,128)S(1)}, u32[]{:S(2)}, u32[]{:S(2)}) %all-to-all-start.1) | async-done | bytes 524320 | tf_op jit(solution)/shard_map/all_to_all | solution.py:210
  105.4 2.1 %shard_map.95 = (f32[2056,128]{1,0:T(8,128)S(1)}, f32[256,128]{1,0:T(8,128)S(1)}) custom-call(s32[1024]{0:T(1024)S(1)} %reshape.56.target, f32[1024,128]{1,0:T(8,128)S(1)} %bitcast.27, f32[2056,128]{1,0:T(8,128)S(1)} %shard_map.93.before, f32[1,128]{1,0:T(1,128)S(1)} %get-tuple-element.42.count), custom_call_target="tpu_custom_call" | custom-call | flops 262144 | bytes 1048576 | tf_op jit(solution)/shard_map/pallas_call | solution.py:222
  107.5 20.3 %all_to_all.20 = f32[256,1,128]{2,1,0:T(1,128)S(1)} all-to-all(f32[256,1,128]{2,1,0:T(1,128)S(1)} %bitcast.29), channel_id=1, replica_groups=mesh['grp'=4,'own_0'=4,'own_1'=8,'own_2'=2] {'grp','own_0','own_1','own_2'}, dimensions={0} | all-to-all | bytes 262144 | tf_op jit(solution)/shard_map/all_to_all | solution.py:229
  127.7 3.4 %shard_map.96 = (f32[2048,128]{1,0:T(8,128)}, f32[2048,128]{1,0:T(8,128)}, f32[2048,128]{1,0:T(8,128)}) custom-call(f32[256,128]{1,0:T(8,128)S(1)} %bitcast.28, f32[2056,128]{1,0:T(8,128)S(1)} %get-tuple-element.44.dense, f32[2056,128]{1,0:T(8,128)S(1)} %get-tuple-element.45.mask, f32[2048,128]{1,0:T(8,128)} %bitcast.34, f32[2048,128]{1,0:T(8,128)} %bitcast.35, ...), custom_call_target="tpu_custom_call" | custom-call | flops 262144 | bytes 1048576 | tf_op jit(solution)/shard_map/pallas_call | solution.py:234
  (3 shorter events, 0.0 us)
Async XLA Ops:
  0.6 7.6 %copy-start = (s32[1,4,64]{2,1,0:T(4,128)S(1)}, s32[1,4,64]{2,1,0:T(4,128)}, u32[]{:S(2)}) copy-start(s32[1,4,64]{2,1,0:T(4,128)} %param.8) | copy-start | bytes 3076
  2.5 12.5 %collective-permute-start.4 = (f32[2,32,16,128]{3,2,1,0:T(8,128)S(1)}, f32[2,32,16,128]{3,2,1,0:T(8,128)S(1)}, u32[]{:S(2)}, u32[]{:S(2)}) collective-permute-start(f32[2,32,16,128]{3,2,1,0:T(8,128)S(1)} %get-tuple-element.36), channel_id=1, source_target_pairs={{0,64},{64,0},{128,192},{192,128},{1,65},{65,1},{129,193},{193,129... | collective-permute-start | bytes 1572872 | tf_op jit(solution)/shard_map/ppermute | solution.py:195
  4.6 13.4 %collective-permute-start.5 = (f32[2,32,16,128]{3,2,1,0:T(8,128)S(1)}, f32[2,32,16,128]{3,2,1,0:T(8,128)S(1)}, u32[]{:S(2)}, u32[]{:S(2)}) collective-permute-start(f32[2,32,16,128]{3,2,1,0:T(8,128)S(1)} %get-tuple-element.37), channel_id=1, source_target_pairs={{0,192},{64,128},{128,64},{192,0},{1,193},{65,129},{129,65},{193,1... | collective-permute-start | bytes 1572872 | tf_op jit(solution)/shard_map/ppermute | solution.py:196
  18.1 17.4 %collective-permute-start.6 = (f32[32,16,128]{2,1,0:T(8,128)S(1)}, f32[32,16,128]{2,1,0:T(8,128)S(1)}, u32[]{:S(2)}, u32[]{:S(2)}) collective-permute-start(f32[32,16,128]{2,1,0:T(8,128)S(1)} %get-tuple-element.40), channel_id=1, source_target_pairs={{0,192},{64,128},{128,64},{192,0},{1,193},{65,129},{129,65},{193,1... | collective-permute-start | bytes 786440 | tf_op jit(solution)/shard_map/ppermute | solution.py:205
  20.3 15.2 %collective-permute-start.7 = (f32[32,16,128]{2,1,0:T(8,128)S(1)}, f32[32,16,128]{2,1,0:T(8,128)S(1)}, u32[]{:S(2)}, u32[]{:S(2)}) collective-permute-start(f32[32,16,128]{2,1,0:T(8,128)S(1)} %get-tuple-element.41), channel_id=1, source_target_pairs={{0,64},{64,0},{128,192},{192,128},{1,65},{65,1},{129,193},{193,129... | collective-permute-start | bytes 786440 | tf_op jit(solution)/shard_map/ppermute | solution.py:206
  21.7 23.0 %all-to-all-start = ((f32[64,1,128]{2,1,0:T(1,128)}), f32[64,1,128]{2,1,0:T(1,128)S(1)}, u32[]{:S(2)}, u32[]{:S(2)}) async-start(f32[64,1,128]{2,1,0:T(1,128)} %copy.10), calls=%async_computation | async-start | bytes 65536 | tf_op jit(solution)/shard_map/all_to_all | solution.py:170
  44.7 30.6 %all-to-all-start.2 = ((f32[64,16,128]{2,1,0:T(8,128)}), f32[64,16,128]{2,1,0:T(8,128)S(1)}, u32[]{:S(2)}, u32[]{:S(2)}) async-start(f32[64,16,128]{2,1,0:T(8,128)} %shard_map.92), calls=%async_computation.2 | async-start | bytes 1048576 | tf_op jit(solution)/shard_map/all_to_all | solution.py:210
  51.2 13.6 %collective-permute-start = (f32[2,32,16,128]{3,2,1,0:T(8,128)S(1)}, f32[2,32,16,128]{3,2,1,0:T(8,128)S(1)}, u32[]{:S(2)}, u32[]{:S(2)}) collective-permute-start(f32[2,32,16,128]{3,2,1,0:T(8,128)S(1)} %get-tuple-element.28), channel_id=1, source_target_pairs={{0,64},{64,0},{128,192},{192,128},{1,65},{65,1},{129,193},{193,129... | collective-permute-start | bytes 1572872 | tf_op jit(solution)/shard_map/ppermute | solution.py:195
  53.1 13.8 %collective-permute-start.1 = (f32[2,32,16,128]{3,2,1,0:T(8,128)S(1)}, f32[2,32,16,128]{3,2,1,0:T(8,128)S(1)}, u32[]{:S(2)}, u32[]{:S(2)}) collective-permute-start(f32[2,32,16,128]{3,2,1,0:T(8,128)S(1)} %get-tuple-element.29), channel_id=1, source_target_pairs={{0,192},{64,128},{128,64},{192,0},{1,193},{65,129},{129,65},{193,1... | collective-permute-start | bytes 1572872 | tf_op jit(solution)/shard_map/ppermute | solution.py:196
  67.0 7.5 %collective-permute-start.2 = (f32[32,16,128]{2,1,0:T(8,128)S(1)}, f32[32,16,128]{2,1,0:T(8,128)S(1)}, u32[]{:S(2)}, u32[]{:S(2)}) collective-permute-start(f32[32,16,128]{2,1,0:T(8,128)S(1)} %get-tuple-element.32), channel_id=1, source_target_pairs={{0,192},{64,128},{128,64},{192,0},{1,193},{65,129},{129,65},{193,1... | collective-permute-start | bytes 786440 | tf_op jit(solution)/shard_map/ppermute | solution.py:205
  67.9 6.5 %collective-permute-start.3 = (f32[32,16,128]{2,1,0:T(8,128)S(1)}, f32[32,16,128]{2,1,0:T(8,128)S(1)}, u32[]{:S(2)}, u32[]{:S(2)}) collective-permute-start(f32[32,16,128]{2,1,0:T(8,128)S(1)} %get-tuple-element.33), channel_id=1, source_target_pairs={{0,64},{64,0},{128,192},{192,128},{1,65},{65,1},{129,193},{193,129... | collective-permute-start | bytes 786440 | tf_op jit(solution)/shard_map/ppermute | solution.py:206
  75.3 30.1 %all-to-all-start.1 = ((f32[64,16,128]{2,1,0:T(8,128)}), f32[64,16,128]{2,1,0:T(8,128)S(1)}, u32[]{:S(2)}, u32[]{:S(2)}) async-start(f32[64,16,128]{2,1,0:T(8,128)} %shard_map.88), calls=%async_computation.1 | async-start | bytes 1048576 | tf_op jit(solution)/shard_map/all_to_all | solution.py:210

commit v3 on v2

--- a/solution.py
+++ b/solution.py
@@ -11,7 +11,7 @@
 
 OWN = ("own_0", "own_1", "own_2")
 GRP_OWN = ("grp", "own_0", "own_1", "own_2")
-CHUNKS = (8, 8)
+CHUNKS = (4, 12)
 STEPS = 4
 f32 = jnp.float32
 ANY = pl.BlockSpec(memory_space=pl.ANY)
@@ -49,14 +49,32 @@
 
 
 def add_kernel(top_own, low_own, top_in, low_in, top_out, low_out):
+    top_out[...] = top_own[...] + top_in[...]
+    low_out[...] = low_own[...] + low_in[...]
+
+
+def sum_kernel(top_own, low_own, top_near, low_near, top_far, low_far, out):
+    half = top_far.shape[0]
+    out[0:half] = top_own[...] + top_near[...] + top_far[...]
+    out[half:] = low_own[...] + low_near[...] + low_far[...]
+
+
+def first_add_kernel(top_own, low_own, top_in, low_in, top_out, low_out):
     top_out[...] = top_own[...] + top_in[1]
     low_out[...] = low_own[...] + low_in[1]
 
 
-def sum_kernel(top_own, low_own, top_near, low_near, top_far, low_far, out):
-    half = top_far.shape[0]
-    out[0:half] = top_own[...] + top_near[0] + top_far[...]
-    out[half:] = low_own[...] + low_near[0] + low_far[...]
+def first_sum_kernel(top_own, low_own, top_near, low_near, top_far, low_far, named, out):
+    half, size = top_far.shape[:2]
+    pitch = out.shape[0] // (2 * half)
+    out[...] = jnp.zeros_like(out)
+    for o in range(half):
+        out[o * pitch : o * pitch + size] = top_own[o] + top_near[0, o] + top_far[o]
+        at = (half + o) * pitch
+        out[at : at + size] = low_own[o] + low_near[0, o] + low_far[o]
+    for o in range(2 * half):
+        at = o * pitch + size
+        out[at : at + 1] = named[o : o + 1]
 
 
 def pair_rows(t):
@@ -76,7 +94,7 @@
     count[...] = jnp.sum(mask[0 : mask.shape[0] - 8], axis=0, keepdims=True)
 
 
-def scatter_rows(slots, first, width, target, rows, even, odd):
+def scatter_rows(slots, first, width, pitch, target, rows, even, odd):
     even[...] = jnp.zeros_like(even)
     odd[...] = jnp.zeros_like(odd)
 
@@ -84,25 +102,23 @@
         picks = []
         for k, ref in ((0, even), (1, odd)):
             for j in range(width):
-                picks.append((ref, target[(2 * s + k) * slots + first + j]))
-        new = [
-            ref[pair_rows(t)] + rows[pair_rows(2 * s * width + j)]
-            for j, (ref, t) in enumerate(picks)
-        ]
-        for (ref, t), value in zip(picks, new):
+                t = target[(2 * s + k) * slots + first + j]
+                picks.append((ref, t, (2 * s + k) * pitch + j))
+        new = [ref[pair_rows(t)] + rows[pair_rows(at)] for ref, t, at in picks]
+        for (ref, t, _), value in zip(picks, new):
             ref[pair_rows(t)] = value
         return carry
 
     lax.fori_loop(0, target.shape[0] // (2 * slots), sources, 0)
 
 
-def first_kernel(slots, width, target, rows, dense, other):
-    scatter_rows(slots, 0, width, target, rows, dense, other)
+def first_kernel(slots, width, pitch, target, rows, dense, other):
+    scatter_rows(slots, 0, width, pitch, target, rows, dense, other)
     dense[...] += other[...]
 
 
 def last_kernel(slots, first, width, target, rows, before, count, dense, message, other):
-    scatter_rows(slots, first, width, target, rows, dense, other)
+    scatter_rows(slots, first, width, width, target, rows, dense, other)
     dense[...] += other[...] + before[...]
     values = dense[0 : dense.shape[0] - 8]
     square = jnp.sum(jnp.sum(values * values, axis=0, keepdims=True), axis=1, keepdims=True)
@@ -166,9 +182,7 @@
     counts = lax.dynamic_index_in_dim(block_counts[0], member, 0, keepdims=False)
     valid = jnp.arange(slots, dtype=jnp.int32)[None, :] < counts[:, None]
     named = jnp.where(valid, ids, blocks).astype(f32)
-    named = jnp.pad(named, ((0, 0), (0, lanes - slots))).reshape(owners, 1, lanes)
-    named = lax.all_to_all(named, OWN, split_axis=0, concat_axis=0, tiled=True)
-    target = named.reshape(owners, lanes)[:, :slots].astype(jnp.int32).reshape(-1)
+    named = jnp.pad(named, ((0, 0), (0, lanes - slots)))
 
     flip, mirror = member ^ 1, 3 - member
     order = jnp.stack([flip, mirror, mirror ^ 1, member])
@@ -186,29 +200,54 @@
         )(order, partial)
 
     spans = [(sum(CHUNKS[:k]) * features, sum(CHUNKS[: k + 1]) * features) for k in (0, 1)]
-    shares = []
-    for span in spans:
-        size = span[1] - span[0]
-        piece, both = shape(half, size, lanes), shape(2, half, size, lanes)
-        plan = ((0, 0, 0, 0, span), (1, 0, 1, 1, span), (0, 1, 2, 0, span), (1, 1, 2, 1, span))
-        top, low = copied((both, both), plan)
-        top_in = lax.ppermute(top, "grp", flips)
-        low_in = lax.ppermute(low, "grp", mirrors)
-        plan = tuple(
-            (n, None, which, part, span)
-            for n, (which, part) in enumerate(((1, 0), (0, 1), (3, 0), (3, 1)))
-        )
-        far_top, far_low, own_top, own_low = copied((piece,) * 4, plan)
-        top, low = kernel_call(add_kernel, (piece, piece), [VMEM] * 4, (VMEM, VMEM))(
-            far_top, far_low, top_in, low_in
-        )
-        top_far = lax.ppermute(top, "grp", mirrors)
-        low_far = lax.ppermute(low, "grp", flips)
-        share = kernel_call(sum_kernel, shape(owners, size, lanes), [VMEM] * 6, VMEM)(
-            own_top, own_low, top_in, low_in, top_far, low_far
-        )
-        share = lax.all_to_all(share, OWN, split_axis=0, concat_axis=0, tiled=True)
-        shares.append(share.reshape(owners * size, lanes))
+
+    def call(body, outs, ins, single=False):
+        specs = VMEM if single else (VMEM,) * len(outs)
+        return kernel_call(body, outs, [VMEM] * len(ins), specs)(*ins)
+
+    def permuted(top, low, top_pairs, low_pairs):
+        return lax.ppermute(top, "grp", top_pairs), lax.ppermute(low, "grp", low_pairs)
+
+    def exchange(share):
+        return lax.all_to_all(share, OWN, split_axis=0, concat_axis=0, tiled=True)
+
+    staged = ((1, 0), (0, 1), (3, 0), (3, 1))
+
+    span = spans[0]
+    size = span[1] - span[0]
+    piece, both = shape(half, size, lanes), shape(2, half, size, lanes)
+    plan = ((0, 0, 0, 0, span), (1, 0, 1, 1, span), (0, 1, 2, 0, span), (1, 1, 2, 1, span))
+    top, low = copied((both, both), plan)
+    near = permuted(top, low, flips, mirrors)
+    plan = tuple((n, None, which, part, span) for n, (which, part) in enumerate(staged))
+    kept = copied((piece,) * 4, plan)
+    ins = (kept[0], kept[1], *near)
+    top, low = call(first_add_kernel, (piece, piece), ins)
+    far = permuted(top, low, mirrors, flips)
+    pitch = size + 2
+    ins = (kept[2], kept[3], *near, *far, named)
+    share = call(first_sum_kernel, shape(owners * pitch, lanes), ins, True)
+    share = exchange(share.reshape(owners, 1, pitch * lanes))
+    named = share[:, 0, size * lanes : size * lanes + slots]
+    target = named.astype(jnp.int32).reshape(-1)
+    shares = [share.reshape(owners * pitch, lanes)]
+
+    span = spans[1]
+    size = span[1] - span[0]
+    piece = shape(half, size, lanes)
+    plan = ((0, None, 2, 0, span), (1, None, 2, 1, span), (2, None, 0, 0, span), (3, None, 1, 1, span))
+    sent = copied((piece,) * 4, plan)
+    late = permuted(sent[0], sent[1], flips, mirrors)
+    near = permuted(sent[2], sent[3], flips, mirrors)
+    plan = tuple((n, None, which, part, span) for n, (which, part) in enumerate(staged))
+    kept = copied((piece,) * 4, plan)
+    ins = (kept[0], kept[1], *late)
+    top, low = call(add_kernel, (piece, piece), ins)
+    far = permuted(top, low, mirrors, flips)
+    ins = (kept[2], kept[3], *near, *far)
+    share = call(sum_kernel, shape(owners, size, lanes), ins, True)
+    share = exchange(share)
+    shares.append(share.reshape(owners * size, lanes))
 
     rows = blocks * features
     table = shape(rows + 8, lanes)
@@ -217,7 +256,7 @@
     )(target)
     spare = [pltpu.VMEM(table.shape, f32)]
     before = kernel_call(
-        functools.partial(first_kernel, slots, CHUNKS[0]), table, [SMEM, VMEM], VMEM, spare
+        functools.partial(first_kernel, slots, CHUNKS[0], pitch // features), table, [SMEM, VMEM], VMEM, spare
     )(target, shares[0])
     dense, message = kernel_call(
         functools.partial(last_kernel, slots, CHUNKS[0], CHUNKS[1]),

time: 132 us -> 120 us (0.909)
  waiting for transfers between devices: 49.2 us -> 42.6 us
  starting transfers between devices: 41.1 us -> 35.2 us
    all_to_all x3 -> x2, starting transfers between devices: 31.3 us -> 25 us  [exchange(): return lax.all_to_all(share, OWN, split_axis=0, concat_axis=0, tiled=True)]
    ppermute x8 -> x10, waiting for transfers between devices: 27.5 us -> 23.4 us  [the longest x5 22.3 us: permuted(): lax.ppermute(top, 'grp', top_pairs)]
    all_to_all x3 -> x2, waiting for transfers between devices: 21.7 us -> 19.2 us  [exchange(): return lax.all_to_all(share, OWN, split_axis=0, concat_axis=0, tiled=True)]
    ppermute x8 -> x10, starting transfers between devices: 9.79 us -> 10.2 us  [the longest x5 5.67 us: permuted(): lax.ppermute(top, 'grp', top_pairs)]
  transfers between devices with their start and end apart: 11 -> 12, of which waited for: 7 -> 5; matrix products, arithmetic and copies ran while one was open for 1% -> 1% of each run, Pallas kernels for 8% -> 10%
where the time goes in v3:
time: 120 us
  waiting for transfers between devices  42.6 us (36%)
  starting transfers between devices  35.2 us (29%)
  blocking collectives  20.5 us (17%)
  Pallas kernels  19.5 us (16%)
    all_to_all x2, starting transfers between devices, exchange(): return lax.all_to_all(share, OWN, split_axis=0, concat_axis=0, tiled=True)  25 us
    ppermute x5, waiting for transfers between devices, permuted(): lax.ppermute(top, 'grp', top_pairs)  22.3 us
    all_to_all x1, blocking collectives, step(): lax.all_to_all(message.reshape(devices, 1, lanes), GRP_OWN, split_axis=0,...  20.5 us
    all_to_all x2, waiting for transfers between devices, exchange(): return lax.all_to_all(share, OWN, split_axis=0, concat_axis=0, tiled=True)  19.2 us
    pallas_call x4, Pallas kernels, copied(): kernel_call(functools.partial(copies_kernel, plan), outs, [SMEM, ANY], (V...  8.22 us
    ppermute x5, starting transfers between devices, permuted(): lax.ppermute(top, 'grp', top_pairs)  5.67 us
    ppermute x5, starting transfers between devices, permuted(): lax.ppermute(low, 'grp', low_pairs)  4.52 us
    pallas_call x1, Pallas kernels, step(): kernel_call(update_kernel, (flat,) * 3, [VMEM] * 3 + [ANY] * 3, (ANY,) *...  3.37 us
  transfers between devices with their start and end apart: 12, of which 5 were waited for; matrix products, arithmetic and copies ran while one was open for 1% of the time, Pallas kernels for 10%

profile of v3, /device:TPU:1, one launch (start us, length us, event | category | flops | bytes accessed | tf_op | source)
XLA Modules:
  0.0 119.7 jit_solution(1848490960146724166)
XLA Ops:
  0.6 0.0 copy-start
  0.7 0.1 pad_add_fusion.order
  0.7 1.7 %shard_map.86 = (f32[2,32,8,128]{3,2,1,0:T(8,128)S(1)}, f32[2,32,8,128]{3,2,1,0:T(8,128)S(1)}) custom-call(s32[4]{0:T(128)S(1)} %pad_add_fusion.order, f32[4,64,32,128]{3,2,1,0:T(8,128)} %bitcast.28), custom_call_target="tpu_custom_call" | custom-call | flops 262144 | bytes 2097152 | tf_op jit(solution)/shard_map/pallas_call | solution.py:193
  2.4 2.1 %collective-permute-start = (f32[2,32,8,128]{3,2,1,0:T(8,128)S(1)}, f32[2,32,8,128]{3,2,1,0:T(8,128)S(1)}, u32[]{:S(2)}, u32[]{:S(2)}) collective-permute-start(f32[2,32,8,128]{3,2,1,0:T(8,128)S(1)} %get-tuple-element.30), channel_id=1, source_target_pairs={{0,64},{64,0},{128,192},{192,128},{1,65},{65,1},{129,193},{193,129... | collective-permute-start | bytes 786440 | tf_op jit(solution)/shard_map/ppermute | solution.py:209
  4.5 1.8 %collective-permute-start.1 = (f32[2,32,8,128]{3,2,1,0:T(8,128)S(1)}, f32[2,32,8,128]{3,2,1,0:T(8,128)S(1)}, u32[]{:S(2)}, u32[]{:S(2)}) collective-permute-start(f32[2,32,8,128]{3,2,1,0:T(8,128)S(1)} %get-tuple-element.31), channel_id=1, source_target_pairs={{0,192},{64,128},{128,64},{192,0},{1,193},{65,129},{129,65},{193,1... | collective-permute-start | bytes 786440 | tf_op jit(solution)/shard_map/ppermute | solution.py:209
  6.3 2.9 %shard_map.90 = (f32[32,24,128]{2,1,0:T(8,128)}, f32[32,24,128]{2,1,0:T(8,128)}, f32[32,24,128]{2,1,0:T(8,128)}, f32[32,24,128]{2,1,0:T(8,128)S(1)}) custom-call(s32[4]{0:T(128)S(1)} %pad_add_fusion.order, f32[4,64,32,128]{3,2,1,0:T(8,128)} %bitcast.29), custom_call_target="tpu_custom_call" | custom-call | flops 262144 | bytes 2097152 | tf_op jit(solution)/shard_map/pallas_call | solution.py:193
  9.3 0.4 collective-permute-start.6
  9.7 0.6 collective-permute-start.7
  10.3 1.7 %shard_map.85 = (f32[32,8,128]{2,1,0:T(8,128)S(1)}, f32[32,8,128]{2,1,0:T(8,128)S(1)}, f32[32,8,128]{2,1,0:T(8,128)S(1)}, f32[32,8,128]{2,1,0:T(8,128)S(1)}) custom-call(s32[4]{0:T(128)S(1)} %pad_add_fusion.order, f32[4,64,32,128]{3,2,1,0:T(8,128)} %bitcast.30), custom_call_target="tpu_custom_call" | custom-call | flops 262144 | bytes 2097152 | tf_op jit(solution)/shard_map/pallas_call | solution.py:193
  12.0 0.0 copy-done
  12.0 0.1 copy.11
  12.1 0.7 dynamic-slice_bitcast_fusion
  12.8 0.0 collective-permute-done.top_in.top_near
  12.8 0.0 collective-permute-done.1.low_in.low_near
  12.9 2.1 %collective-permute-start.2 = (f32[32,8,128]{2,1,0:T(8,128)S(1)}, f32[32,8,128]{2,1,0:T(8,128)S(1)}, u32[]{:S(2)}, u32[]{:S(2)}) collective-permute-start(f32[32,8,128]{2,1,0:T(8,128)S(1)} %get-tuple-element.34), channel_id=1, source_target_pairs={{0,192},{64,128},{128,64},{192,0},{1,193},{65,129},{129,65},{193,1... | collective-permute-start | bytes 393224 | tf_op jit(solution)/shard_map/ppermute | solution.py:209
  15.0 0.0 collective-permute-start.3
  15.0 0.1 fusion.1
  15.1 8.5 %collective-permute-done.2.top_far = f32[32,8,128]{2,1,0:T(8,128)S(1)} collective-permute-done((f32[32,8,128]{2,1,0:T(8,128)S(1)}, f32[32,8,128]{2,1,0:T(8,128)S(1)}, u32[]{:S(2)}, u32[]{:S(2)}) %collective-permute-start.2) | collective-permute-done | bytes 131104 | tf_op jit(solution)/shard_map/ppermute | solution.py:209
  23.6 0.0 collective-permute-done.3.low_far
  23.6 0.8 shard_map.88
  24.4 13.8 %all-to-all-start = ((f32[64,1,1280]{2,1,0:T(1,128)}), f32[64,1,1280]{2,1,0:T(1,128)S(1)}, u32[]{:S(2)}, u32[]{:S(2)}) async-start(f32[64,1,1280]{2,1,0:T(1,128)} %bitcast.7), calls=%async_computation | async-start | bytes 655360 | tf_op jit(solution)/shard_map/all_to_all | solution.py:212
  38.2 0.1 collective-permute-start.4
  38.3 1.9 %collective-permute-start.5 = (f32[32,24,128]{2,1,0:T(8,128)S(1)}, f32[32,24,128]{2,1,0:T(8,128)S(1)}, u32[]{:S(2)}, u32[]{:S(2)}) collective-permute-start(f32[32,24,128]{2,1,0:T(8,128)S(1)} %get-tuple-element.39), channel_id=1, source_target_pairs={{0,192},{64,128},{128,64},{192,0},{1,193},{65,129},{129,65},{193,1... | collective-permute-start | bytes 1179656 | tf_op jit(solution)/shard_map/ppermute | solution.py:209
  40.2 1.9 %shard_map.89 = (f32[32,24,128]{2,1,0:T(8,128)S(1)}, f32[32,24,128]{2,1,0:T(8,128)S(1)}, f32[32,24,128]{2,1,0:T(8,128)S(1)}, f32[32,24,128]{2,1,0:T(8,128)S(1)}) custom-call(s32[4]{0:T(128)S(1)} %pad_add_fusion.order, f32[4,64,32,128]{3,2,1,0:T(8,128)} %bitcast.31), custom_call_target="tpu_custom_call" | custom-call | flops 262144 | bytes 2097152 | tf_op jit(solution)/shard_map/pallas_call | solution.py:193
  42.1 0.0 collective-permute-done.6.top_in
  42.1 0.0 collective-permute-done.7.low_in
  42.1 0.1 shard_map.91
  42.2 0.9 collective-permute-start.8
  43.2 0.2 collective-permute-start.9
  43.3 5.4 %collective-permute-done.4.top_near = f32[32,24,128]{2,1,0:T(8,128)S(1)} collective-permute-done((f32[32,24,128]{2,1,0:T(8,128)}, f32[32,24,128]{2,1,0:T(8,128)S(1)}, u32[]{:S(2)}, u32[]{:S(2)}) %collective-permute-start.4) | collective-permute-done | bytes 393248 | tf_op jit(solution)/shard_map/ppermute | solution.py:209
  48.7 1.1 collective-permute-done.5.low_near
  49.8 8.4 %collective-permute-done.8.top_far = f32[32,24,128]{2,1,0:T(8,128)S(1)} collective-permute-done((f32[32,24,128]{2,1,0:T(8,128)S(1)}, f32[32,24,128]{2,1,0:T(8,128)S(1)}, u32[]{:S(2)}, u32[]{:S(2)}) %collective-permute-start.8) | collective-permute-done | bytes 393248 | tf_op jit(solution)/shard_map/ppermute | solution.py:209
  58.2 0.0 collective-permute-done.9.low_far
  58.2 1.0 shard_map.92
  59.2 0.0 all-to-all-done
  59.2 11.2 %all-to-all-start.1 = ((f32[64,24,128]{2,1,0:T(8,128)}), f32[64,24,128]{2,1,0:T(8,128)S(1)}, u32[]{:S(2)}, u32[]{:S(2)}) async-start(f32[64,24,128]{2,1,0:T(8,128)} %shard_map.92), calls=%async_computation.1 | async-start | bytes 1572864 | tf_op jit(solution)/shard_map/all_to_all | solution.py:212
  70.5 0.1 fusion
  70.6 0.1 convert_element_type.14.target
  70.6 2.3 %shard_map.94 = (f32[2056,128]{1,0:T(8,128)S(1)}, f32[1,128]{1,0:T(1,128)S(1)}) custom-call(s32[1024]{0:T(1024)S(1)} %convert_element_type.14.target), custom_call_target="tpu_custom_call" | custom-call | flops 262144 | bytes 1048576 | tf_op jit(solution)/shard_map/pallas_call | solution.py:254
  72.9 1.3 %shard_map.93.before = f32[2056,128]{1,0:T(8,128)S(1)} custom-call(s32[1024]{0:T(1024)S(1)} %convert_element_type.14.target, f32[640,128]{1,0:T(8,128)S(1)} %bitcast.25), custom_call_target="tpu_custom_call" | custom-call | flops 262144 | bytes 1048576 | tf_op jit(solution)/shard_map/pallas_call | solution.py:258
  74.2 19.2 %all-to-all-done.1 = f32[64,24,128]{2,1,0:T(8,128)S(1)} async-done(((f32[64,24,128]{2,1,0:T(8,128)}), f32[64,24,128]{2,1,0:T(8,128)S(1)}, u32[]{:S(2)}, u32[]{:S(2)}) %all-to-all-start.1) | async-done | bytes 786464 | tf_op jit(solution)/shard_map/all_to_all | solution.py:212
  93.4 2.4 %shard_map.95 = (f32[2056,128]{1,0:T(8,128)S(1)}, f32[256,128]{1,0:T(8,128)S(1)}) custom-call(s32[1024]{0:T(1024)S(1)} %convert_element_type.14.target, f32[1536,128]{1,0:T(8,128)S(1)} %bitcast.24, f32[2056,128]{1,0:T(8,128)S(1)} %shard_map.93.before, f32[1,128]{1,0:T(1,128)S(1)} %get-tuple-element.46.count), custom_call_target="tpu_custom_call" | custom-call | flops 262144 | bytes 1048576 | tf_op jit(solution)/shard_map/pallas_call | solution.py:261
  95.8 20.5 %all_to_all.15 = f32[256,1,128]{2,1,0:T(1,128)S(1)} all-to-all(f32[256,1,128]{2,1,0:T(1,128)S(1)} %bitcast.27), channel_id=1, replica_groups=mesh['grp'=4,'own_0'=4,'own_1'=8,'own_2'=2] {'grp','own_0','own_1','own_2'}, dimensions={0} | all-to-all | bytes 262144 | tf_op jit(solution)/shard_map/all_to_all | solution.py:268
  116.4 3.4 %shard_map.96 = (f32[2048,128]{1,0:T(8,128)}, f32[2048,128]{1,0:T(8,128)}, f32[2048,128]{1,0:T(8,128)}) custom-call(f32[256,128]{1,0:T(8,128)S(1)} %bitcast.26, f32[2056,128]{1,0:T(8,128)S(1)} %get-tuple-element.48.dense, f32[2056,128]{1,0:T(8,128)S(1)} %get-tuple-element.49.mask, f32[2048,128]{1,0:T(8,128)} %bitcast.32, f32[2048,128]{1,0:T(8,128)} %bitcast.33, ...), custom_call_target="tpu_custom_call" | custom-call | flops 262144 | bytes 1048576 | tf_op jit(solution)/shard_map/pallas_call | solution.py:273
  (3 shorter events, 0.0 us)
Async XLA Ops:
  0.6 11.4 %copy-start = (s32[1,4,64,16]{2,3,1,0:T(8,128)S(1)}, s32[1,4,64,16]{2,3,1,0:T(8,128)}, u32[]{:S(2)}) copy-start(s32[1,4,64,16]{2,3,1,0:T(8,128)} %param.7) | copy-start | bytes 49156
  2.4 10.4 %collective-permute-start = (f32[2,32,8,128]{3,2,1,0:T(8,128)S(1)}, f32[2,32,8,128]{3,2,1,0:T(8,128)S(1)}, u32[]{:S(2)}, u32[]{:S(2)}) collective-permute-start(f32[2,32,8,128]{3,2,1,0:T(8,128)S(1)} %get-tuple-element.30), channel_id=1, source_target_pairs={{0,64},{64,0},{128,192},{192,128},{1,65},{65,1},{129,193},{193,129... | collective-permute-start | bytes 786440 | tf_op jit(solution)/shard_map/ppermute | solution.py:209
  4.5 8.3 %collective-permute-start.1 = (f32[2,32,8,128]{3,2,1,0:T(8,128)S(1)}, f32[2,32,8,128]{3,2,1,0:T(8,128)S(1)}, u32[]{:S(2)}, u32[]{:S(2)}) collective-permute-start(f32[2,32,8,128]{3,2,1,0:T(8,128)S(1)} %get-tuple-element.31), channel_id=1, source_target_pairs={{0,192},{64,128},{128,64},{192,0},{1,193},{65,129},{129,65},{193,1... | collective-permute-start | bytes 786440 | tf_op jit(solution)/shard_map/ppermute | solution.py:209
  9.3 32.8 %collective-permute-start.6 = (f32[32,24,128]{2,1,0:T(8,128)}, f32[32,24,128]{2,1,0:T(8,128)S(1)}, u32[]{:S(2)}, u32[]{:S(2)}) collective-permute-start(f32[32,24,128]{2,1,0:T(8,128)} %get-tuple-element.42), channel_id=1, source_target_pairs={{0,64},{64,0},{128,192},{192,128},{1,65},{65,1},{129,193},{193,129... | collective-permute-start | bytes 1179656 | tf_op jit(solution)/shard_map/ppermute | solution.py:209
  9.7 32.4 %collective-permute-start.7 = (f32[32,24,128]{2,1,0:T(8,128)}, f32[32,24,128]{2,1,0:T(8,128)S(1)}, u32[]{:S(2)}, u32[]{:S(2)}) collective-permute-start(f32[32,24,128]{2,1,0:T(8,128)} %get-tuple-element.43), channel_id=1, source_target_pairs={{0,192},{64,128},{128,64},{192,0},{1,193},{65,129},{129,65},{193,1... | collective-permute-start | bytes 1179656 | tf_op jit(solution)/shard_map/ppermute | solution.py:209
  12.9 10.7 %collective-permute-start.2 = (f32[32,8,128]{2,1,0:T(8,128)S(1)}, f32[32,8,128]{2,1,0:T(8,128)S(1)}, u32[]{:S(2)}, u32[]{:S(2)}) collective-permute-start(f32[32,8,128]{2,1,0:T(8,128)S(1)} %get-tuple-element.34), channel_id=1, source_target_pairs={{0,192},{64,128},{128,64},{192,0},{1,193},{65,129},{129,65},{193,1... | collective-permute-start | bytes 393224 | tf_op jit(solution)/shard_map/ppermute | solution.py:209
  15.0 8.6 %collective-permute-start.3 = (f32[32,8,128]{2,1,0:T(8,128)S(1)}, f32[32,8,128]{2,1,0:T(8,128)S(1)}, u32[]{:S(2)}, u32[]{:S(2)}) collective-permute-start(f32[32,8,128]{2,1,0:T(8,128)S(1)} %get-tuple-element.35), channel_id=1, source_target_pairs={{0,64},{64,0},{128,192},{192,128},{1,65},{65,1},{129,193},{193,129... | collective-permute-start | bytes 393224 | tf_op jit(solution)/shard_map/ppermute | solution.py:209
  24.4 34.8 %all-to-all-start = ((f32[64,1,1280]{2,1,0:T(1,128)}), f32[64,1,1280]{2,1,0:T(1,128)S(1)}, u32[]{:S(2)}, u32[]{:S(2)}) async-start(f32[64,1,1280]{2,1,0:T(1,128)} %bitcast.7), calls=%async_computation | async-start | bytes 655360 | tf_op jit(solution)/shard_map/all_to_all | solution.py:212
  38.2 10.5 %collective-permute-start.4 = (f32[32,24,128]{2,1,0:T(8,128)}, f32[32,24,128]{2,1,0:T(8,128)S(1)}, u32[]{:S(2)}, u32[]{:S(2)}) collective-permute-start(f32[32,24,128]{2,1,0:T(8,128)} %get-tuple-element.38), channel_id=1, source_target_pairs={{0,64},{64,0},{128,192},{192,128},{1,65},{65,1},{129,193},{193,129... | collective-permute-start | bytes 1179656 | tf_op jit(solution)/shard_map/ppermute | solution.py:209
  38.3 11.5 %collective-permute-start.5 = (f32[32,24,128]{2,1,0:T(8,128)S(1)}, f32[32,24,128]{2,1,0:T(8,128)S(1)}, u32[]{:S(2)}, u32[]{:S(2)}) collective-permute-start(f32[32,24,128]{2,1,0:T(8,128)S(1)} %get-tuple-element.39), channel_id=1, source_target_pairs={{0,192},{64,128},{128,64},{192,0},{1,193},{65,129},{129,65},{193,1... | collective-permute-start | bytes 1179656 | tf_op jit(solution)/shard_map/ppermute | solution.py:209
  42.2 16.0 %collective-permute-start.8 = (f32[32,24,128]{2,1,0:T(8,128)S(1)}, f32[32,24,128]{2,1,0:T(8,128)S(1)}, u32[]{:S(2)}, u32[]{:S(2)}) collective-permute-start(f32[32,24,128]{2,1,0:T(8,128)S(1)} %get-tuple-element.44), channel_id=1, source_target_pairs={{0,192},{64,128},{128,64},{192,0},{1,193},{65,129},{129,65},{193,1... | collective-permute-start | bytes 1179656 | tf_op jit(solution)/shard_map/ppermute | solution.py:209
  43.2 15.0 %collective-permute-start.9 = (f32[32,24,128]{2,1,0:T(8,128)S(1)}, f32[32,24,128]{2,1,0:T(8,128)S(1)}, u32[]{:S(2)}, u32[]{:S(2)}) collective-permute-start(f32[32,24,128]{2,1,0:T(8,128)S(1)} %get-tuple-element.45), channel_id=1, source_target_pairs={{0,64},{64,0},{128,192},{192,128},{1,65},{65,1},{129,193},{193,129... | collective-permute-start | bytes 1179656 | tf_op jit(solution)/shard_map/ppermute | solution.py:209
  59.2 34.2 %all-to-all-start.1 = ((f32[64,24,128]{2,1,0:T(8,128)}), f32[64,24,128]{2,1,0:T(8,128)S(1)}, u32[]{:S(2)}, u32[]{:S(2)}) async-start(f32[64,24,128]{2,1,0:T(8,128)} %shard_map.92), calls=%async_computation.1 | async-start | bytes 1572864 | tf_op jit(solution)/shard_map/all_to_all | solution.py:212

commit v4 on v3

--- a/solution.py
+++ b/solution.py
@@ -235,10 +235,10 @@
     span = spans[1]
     size = span[1] - span[0]
     piece = shape(half, size, lanes)
-    plan = ((0, None, 2, 0, span), (1, None, 2, 1, span), (2, None, 0, 0, span), (3, None, 1, 1, span))
-    sent = copied((piece,) * 4, plan)
-    late = permuted(sent[0], sent[1], flips, mirrors)
-    near = permuted(sent[2], sent[3], flips, mirrors)
+    sent = copied((piece,) * 2, ((0, None, 2, 0, span), (1, None, 2, 1, span)))
+    late = permuted(*sent, flips, mirrors)
+    sent = copied((piece,) * 2, ((0, None, 0, 0, span), (1, None, 1, 1, span)))
+    near = permuted(*sent, flips, mirrors)
     plan = tuple((n, None, which, part, span) for n, (which, part) in enumerate(staged))
     kept = copied((piece,) * 4, plan)
     ins = (kept[0], kept[1], *late)

time: 120 us -> 122 us (1.017)
    pallas_call x4 -> x5, Pallas kernels: 8.22 us -> 9.38 us  [copied(): kernel_call(functools.partial(copies_kernel, plan), outs, [SMEM, ANY], (V...]
  transfers between devices with their start and end apart: 12 -> 12, of which waited for: 5 -> 5; matrix products, arithmetic and copies ran while one was open for 1% -> 1% of each run, Pallas kernels for 10% -> 11%
where the time goes in v4:
time: 122 us; the launch traced here: 121 us
  waiting for transfers between devices  43.7 us (36%)
  starting transfers between devices  34.6 us (28%)
  Pallas kernels  20.6 us (17%)
  blocking collectives  20.5 us (17%)
    all_to_all x2, starting transfers between devices, exchange(): return lax.all_to_all(share, OWN, split_axis=0, concat_axis=0, tiled=True)  24.3 us
    ppermute x5, waiting for transfers between devices, permuted(): lax.ppermute(top, 'grp', top_pairs)  23.2 us
    all_to_all x1, blocking collectives, step(): lax.all_to_all(message.reshape(devices, 1, lanes), GRP_OWN, split_axis=0,...  20.5 us
    all_to_all x2, waiting for transfers between devices, exchange(): return lax.all_to_all(share, OWN, split_axis=0, concat_axis=0, tiled=True)  19.2 us
    pallas_call x5, Pallas kernels, copied(): kernel_call(functools.partial(copies_kernel, plan), outs, [SMEM, ANY], (V...  9.38 us
    ppermute x5, starting transfers between devices, permuted(): lax.ppermute(top, 'grp', top_pairs)  5.78 us
    ppermute x5, starting transfers between devices, permuted(): lax.ppermute(low, 'grp', low_pairs)  4.52 us
    pallas_call x1, Pallas kernels, step(): kernel_call(update_kernel, (flat,) * 3, [VMEM] * 3 + [ANY] * 3, (ANY,) *...  3.37 us
  transfers between devices with their start and end apart: 12, of which 5 were waited for; matrix products, arithmetic and copies ran while one was open for 1% of the time, Pallas kernels for 11%

profile of v4, /device:TPU:1, one launch (start us, length us, event | category | flops | bytes accessed | tf_op | source)
XLA Modules:
  0.0 121.4 jit_solution(8422837662326837257)
XLA Ops:
  0.6 0.0 copy-start
  0.7 0.1 pad_add_fusion.order
  0.7 1.7 %shard_map.86 = (f32[2,32,8,128]{3,2,1,0:T(8,128)S(1)}, f32[2,32,8,128]{3,2,1,0:T(8,128)S(1)}) custom-call(s32[4]{0:T(128)S(1)} %pad_add_fusion.order, f32[4,64,32,128]{3,2,1,0:T(8,128)} %bitcast.28), custom_call_target="tpu_custom_call" | custom-call | flops 262144 | bytes 2097152 | tf_op jit(solution)/shard_map/pallas_call | solution.py:193
  2.4 2.1 %collective-permute-start = (f32[2,32,8,128]{3,2,1,0:T(8,128)S(1)}, f32[2,32,8,128]{3,2,1,0:T(8,128)S(1)}, u32[]{:S(2)}, u32[]{:S(2)}) collective-permute-start(f32[2,32,8,128]{3,2,1,0:T(8,128)S(1)} %get-tuple-element.30), channel_id=1, source_target_pairs={{0,64},{64,0},{128,192},{192,128},{1,65},{65,1},{129,193},{193,129... | collective-permute-start | bytes 786440 | tf_op jit(solution)/shard_map/ppermute | solution.py:209
  4.5 1.8 %collective-permute-start.1 = (f32[2,32,8,128]{3,2,1,0:T(8,128)S(1)}, f32[2,32,8,128]{3,2,1,0:T(8,128)S(1)}, u32[]{:S(2)}, u32[]{:S(2)}) collective-permute-start(f32[2,32,8,128]{3,2,1,0:T(8,128)S(1)} %get-tuple-element.31), channel_id=1, source_target_pairs={{0,192},{64,128},{128,64},{192,0},{1,193},{65,129},{129,65},{193,1... | collective-permute-start | bytes 786440 | tf_op jit(solution)/shard_map/ppermute | solution.py:209
  6.3 2.4 %shard_map.91 = (f32[32,24,128]{2,1,0:T(8,128)}, f32[32,24,128]{2,1,0:T(8,128)S(1)}) custom-call(s32[4]{0:T(128)S(1)} %pad_add_fusion.order, f32[4,64,32,128]{3,2,1,0:T(8,128)} %bitcast.29), custom_call_target="tpu_custom_call" | custom-call | flops 262144 | bytes 1048576 | tf_op jit(solution)/shard_map/pallas_call | solution.py:193
  8.8 0.4 collective-permute-start.6
  9.2 0.6 collective-permute-start.7
  9.8 1.7 %shard_map.85 = (f32[32,8,128]{2,1,0:T(8,128)S(1)}, f32[32,8,128]{2,1,0:T(8,128)S(1)}, f32[32,8,128]{2,1,0:T(8,128)S(1)}, f32[32,8,128]{2,1,0:T(8,128)S(1)}) custom-call(s32[4]{0:T(128)S(1)} %pad_add_fusion.order, f32[4,64,32,128]{3,2,1,0:T(8,128)} %bitcast.30), custom_call_target="tpu_custom_call" | custom-call | flops 262144 | bytes 2097152 | tf_op jit(solution)/shard_map/pallas_call | solution.py:193
  11.5 0.0 copy-done
  11.5 0.1 copy.11
  11.6 0.7 dynamic-slice_bitcast_fusion
  12.3 0.0 collective-permute-done.top_in.top_near
  12.3 0.0 collective-permute-done.1.low_in.low_near
  12.4 2.2 %collective-permute-start.2 = (f32[32,8,128]{2,1,0:T(8,128)S(1)}, f32[32,8,128]{2,1,0:T(8,128)S(1)}, u32[]{:S(2)}, u32[]{:S(2)}) collective-permute-start(f32[32,8,128]{2,1,0:T(8,128)S(1)} %get-tuple-element.34), channel_id=1, source_target_pairs={{0,192},{64,128},{128,64},{192,0},{1,193},{65,129},{129,65},{193,1... | collective-permute-start | bytes 393224 | tf_op jit(solution)/shard_map/ppermute | solution.py:209
  14.6 0.0 collective-permute-start.3
  14.6 0.1 fusion.1
  14.7 9.6 %collective-permute-done.2.top_far = f32[32,8,128]{2,1,0:T(8,128)S(1)} collective-permute-done((f32[32,8,128]{2,1,0:T(8,128)S(1)}, f32[32,8,128]{2,1,0:T(8,128)S(1)}, u32[]{:S(2)}, u32[]{:S(2)}) %collective-permute-start.2) | collective-permute-done | bytes 131104 | tf_op jit(solution)/shard_map/ppermute | solution.py:209
  24.3 0.0 collective-permute-done.3.low_far
  24.3 0.8 shard_map.88
  25.1 13.0 %all-to-all-start = ((f32[64,1,1280]{2,1,0:T(1,128)}), f32[64,1,1280]{2,1,0:T(1,128)S(1)}, u32[]{:S(2)}, u32[]{:S(2)}) async-start(f32[64,1,1280]{2,1,0:T(1,128)} %bitcast.7), calls=%async_computation | async-start | bytes 655360 | tf_op jit(solution)/shard_map/all_to_all | solution.py:212
  38.2 1.7 %shard_map.90 = (f32[32,24,128]{2,1,0:T(8,128)S(1)}, f32[32,24,128]{2,1,0:T(8,128)S(1)}) custom-call(s32[4]{0:T(128)S(1)} %pad_add_fusion.order, f32[4,64,32,128]{3,2,1,0:T(8,128)} %bitcast.31), custom_call_target="tpu_custom_call" | custom-call | flops 262144 | bytes 1048576 | tf_op jit(solution)/shard_map/pallas_call | solution.py:193
  39.8 0.1 collective-permute-start.4
  39.9 1.9 %collective-permute-start.5 = (f32[32,24,128]{2,1,0:T(8,128)S(1)}, f32[32,24,128]{2,1,0:T(8,128)S(1)}, u32[]{:S(2)}, u32[]{:S(2)}) collective-permute-start(f32[32,24,128]{2,1,0:T(8,128)S(1)} %get-tuple-element.39), channel_id=1, source_target_pairs={{0,192},{64,128},{128,64},{192,0},{1,193},{65,129},{129,65},{193,1... | collective-permute-start | bytes 1179656 | tf_op jit(solution)/shard_map/ppermute | solution.py:209
  41.8 1.9 %shard_map.89 = (f32[32,24,128]{2,1,0:T(8,128)S(1)}, f32[32,24,128]{2,1,0:T(8,128)S(1)}, f32[32,24,128]{2,1,0:T(8,128)S(1)}, f32[32,24,128]{2,1,0:T(8,128)S(1)}) custom-call(s32[4]{0:T(128)S(1)} %pad_add_fusion.order, f32[4,64,32,128]{3,2,1,0:T(8,128)} %bitcast.32), custom_call_target="tpu_custom_call" | custom-call | flops 262144 | bytes 2097152 | tf_op jit(solution)/shard_map/pallas_call | solution.py:193
  43.8 0.0 collective-permute-done.6.top_in
  43.8 0.0 collective-permute-done.7.low_in
  43.8 0.1 shard_map.92
  43.9 0.9 collective-permute-start.8
  44.8 0.2 collective-permute-start.9
  45.0 5.2 %collective-permute-done.4.top_near = f32[32,24,128]{2,1,0:T(8,128)S(1)} collective-permute-done((f32[32,24,128]{2,1,0:T(8,128)S(1)}, f32[32,24,128]{2,1,0:T(8,128)S(1)}, u32[]{:S(2)}, u32[]{:S(2)}) %collective-permute-start.4) | collective-permute-done | bytes 393248 | tf_op jit(solution)/shard_map/ppermute | solution.py:209
  50.1 1.3 %collective-permute-done.5.low_near = f32[32,24,128]{2,1,0:T(8,128)S(1)} collective-permute-done((f32[32,24,128]{2,1,0:T(8,128)S(1)}, f32[32,24,128]{2,1,0:T(8,128)S(1)}, u32[]{:S(2)}, u32[]{:S(2)}) %collective-permute-start.5) | collective-permute-done | bytes 393248 | tf_op jit(solution)/shard_map/ppermute | solution.py:209
  51.5 8.4 %collective-permute-done.8.top_far = f32[32,24,128]{2,1,0:T(8,128)S(1)} collective-permute-done((f32[32,24,128]{2,1,0:T(8,128)S(1)}, f32[32,24,128]{2,1,0:T(8,128)S(1)}, u32[]{:S(2)}, u32[]{:S(2)}) %collective-permute-start.8) | collective-permute-done | bytes 393248 | tf_op jit(solution)/shard_map/ppermute | solution.py:209
  59.9 0.0 collective-permute-done.9.low_far
  59.9 1.0 shard_map.93
  60.9 0.0 all-to-all-done
  60.9 11.2 %all-to-all-start.1 = ((f32[64,24,128]{2,1,0:T(8,128)}), f32[64,24,128]{2,1,0:T(8,128)S(1)}, u32[]{:S(2)}, u32[]{:S(2)}) async-start(f32[64,24,128]{2,1,0:T(8,128)} %shard_map.93), calls=%async_computation.1 | async-start | bytes 1572864 | tf_op jit(solution)/shard_map/all_to_all | solution.py:212
  72.1 0.1 fusion
  72.2 0.1 convert_element_type.14.target
  72.3 2.3 %shard_map.95 = (f32[2056,128]{1,0:T(8,128)S(1)}, f32[1,128]{1,0:T(1,128)S(1)}) custom-call(s32[1024]{0:T(1024)S(1)} %convert_element_type.14.target), custom_call_target="tpu_custom_call" | custom-call | flops 262144 | bytes 1048576 | tf_op jit(solution)/shard_map/pallas_call | solution.py:254
  74.6 1.3 %shard_map.94.before = f32[2056,128]{1,0:T(8,128)S(1)} custom-call(s32[1024]{0:T(1024)S(1)} %convert_element_type.14.target, f32[640,128]{1,0:T(8,128)S(1)} %bitcast.25), custom_call_target="tpu_custom_call" | custom-call | flops 262144 | bytes 1048576 | tf_op jit(solution)/shard_map/pallas_call | solution.py:258
  75.9 19.2 %all-to-all-done.1 = f32[64,24,128]{2,1,0:T(8,128)S(1)} async-done(((f32[64,24,128]{2,1,0:T(8,128)}), f32[64,24,128]{2,1,0:T(8,128)S(1)}, u32[]{:S(2)}, u32[]{:S(2)}) %all-to-all-start.1) | async-done | bytes 786464 | tf_op jit(solution)/shard_map/all_to_all | solution.py:212
  95.1 2.4 %shard_map.96 = (f32[2056,128]{1,0:T(8,128)S(1)}, f32[256,128]{1,0:T(8,128)S(1)}) custom-call(s32[1024]{0:T(1024)S(1)} %convert_element_type.14.target, f32[1536,128]{1,0:T(8,128)S(1)} %bitcast.24, f32[2056,128]{1,0:T(8,128)S(1)} %shard_map.94.before, f32[1,128]{1,0:T(1,128)S(1)} %get-tuple-element.46.count), custom_call_target="tpu_custom_call" | custom-call | flops 262144 | bytes 1048576 | tf_op jit(solution)/shard_map/pallas_call | solution.py:261
  97.5 20.5 %all_to_all.15 = f32[256,1,128]{2,1,0:T(1,128)S(1)} all-to-all(f32[256,1,128]{2,1,0:T(1,128)S(1)} %bitcast.27), channel_id=1, replica_groups=mesh['grp'=4,'own_0'=4,'own_1'=8,'own_2'=2] {'grp','own_0','own_1','own_2'}, dimensions={0} | all-to-all | bytes 262144 | tf_op jit(solution)/shard_map/all_to_all | solution.py:268
  118.0 3.4 %shard_map.97 = (f32[2048,128]{1,0:T(8,128)}, f32[2048,128]{1,0:T(8,128)}, f32[2048,128]{1,0:T(8,128)}) custom-call(f32[256,128]{1,0:T(8,128)S(1)} %bitcast.26, f32[2056,128]{1,0:T(8,128)S(1)} %get-tuple-element.48.dense, f32[2056,128]{1,0:T(8,128)S(1)} %get-tuple-element.49.mask, f32[2048,128]{1,0:T(8,128)} %bitcast.33, f32[2048,128]{1,0:T(8,128)} %bitcast.34, ...), custom_call_target="tpu_custom_call" | custom-call | flops 262144 | bytes 1048576 | tf_op jit(solution)/shard_map/pallas_call | solution.py:273
  (3 shorter events, 0.0 us)
Async XLA Ops:
  0.6 10.9 %copy-start = (s32[1,4,64,16]{2,3,1,0:T(8,128)S(1)}, s32[1,4,64,16]{2,3,1,0:T(8,128)}, u32[]{:S(2)}) copy-start(s32[1,4,64,16]{2,3,1,0:T(8,128)} %param.7) | copy-start | bytes 49156
  2.4 9.9 %collective-permute-start = (f32[2,32,8,128]{3,2,1,0:T(8,128)S(1)}, f32[2,32,8,128]{3,2,1,0:T(8,128)S(1)}, u32[]{:S(2)}, u32[]{:S(2)}) collective-permute-start(f32[2,32,8,128]{3,2,1,0:T(8,128)S(1)} %get-tuple-element.30), channel_id=1, source_target_pairs={{0,64},{64,0},{128,192},{192,128},{1,65},{65,1},{129,193},{193,129... | collective-permute-start | bytes 786440 | tf_op jit(solution)/shard_map/ppermute | solution.py:209
  4.5 7.8 %collective-permute-start.1 = (f32[2,32,8,128]{3,2,1,0:T(8,128)S(1)}, f32[2,32,8,128]{3,2,1,0:T(8,128)S(1)}, u32[]{:S(2)}, u32[]{:S(2)}) collective-permute-start(f32[2,32,8,128]{3,2,1,0:T(8,128)S(1)} %get-tuple-element.31), channel_id=1, source_target_pairs={{0,192},{64,128},{128,64},{192,0},{1,193},{65,129},{129,65},{193,1... | collective-permute-start | bytes 786440 | tf_op jit(solution)/shard_map/ppermute | solution.py:209
  8.8 35.0 %collective-permute-start.6 = (f32[32,24,128]{2,1,0:T(8,128)}, f32[32,24,128]{2,1,0:T(8,128)S(1)}, u32[]{:S(2)}, u32[]{:S(2)}) collective-permute-start(f32[32,24,128]{2,1,0:T(8,128)} %get-tuple-element.42), channel_id=1, source_target_pairs={{0,64},{64,0},{128,192},{192,128},{1,65},{65,1},{129,193},{193,129... | collective-permute-start | bytes 1179656 | tf_op jit(solution)/shard_map/ppermute | solution.py:209
  9.2 34.6 %collective-permute-start.7 = (f32[32,24,128]{2,1,0:T(8,128)S(1)}, f32[32,24,128]{2,1,0:T(8,128)S(1)}, u32[]{:S(2)}, u32[]{:S(2)}) collective-permute-start(f32[32,24,128]{2,1,0:T(8,128)S(1)} %get-tuple-element.43), channel_id=1, source_target_pairs={{0,192},{64,128},{128,64},{192,0},{1,193},{65,129},{129,65},{193,1... | collective-permute-start | bytes 1179656 | tf_op jit(solution)/shard_map/ppermute | solution.py:209
  12.4 11.9 %collective-permute-start.2 = (f32[32,8,128]{2,1,0:T(8,128)S(1)}, f32[32,8,128]{2,1,0:T(8,128)S(1)}, u32[]{:S(2)}, u32[]{:S(2)}) collective-permute-start(f32[32,8,128]{2,1,0:T(8,128)S(1)} %get-tuple-element.34), channel_id=1, source_target_pairs={{0,192},{64,128},{128,64},{192,0},{1,193},{65,129},{129,65},{193,1... | collective-permute-start | bytes 393224 | tf_op jit(solution)/shard_map/ppermute | solution.py:209
  14.6 9.7 %collective-permute-start.3 = (f32[32,8,128]{2,1,0:T(8,128)S(1)}, f32[32,8,128]{2,1,0:T(8,128)S(1)}, u32[]{:S(2)}, u32[]{:S(2)}) collective-permute-start(f32[32,8,128]{2,1,0:T(8,128)S(1)} %get-tuple-element.35), channel_id=1, source_target_pairs={{0,64},{64,0},{128,192},{192,128},{1,65},{65,1},{129,193},{193,129... | collective-permute-start | bytes 393224 | tf_op jit(solution)/shard_map/ppermute | solution.py:209
  25.1 35.8 %all-to-all-start = ((f32[64,1,1280]{2,1,0:T(1,128)}), f32[64,1,1280]{2,1,0:T(1,128)S(1)}, u32[]{:S(2)}, u32[]{:S(2)}) async-start(f32[64,1,1280]{2,1,0:T(1,128)} %bitcast.7), calls=%async_computation | async-start | bytes 655360 | tf_op jit(solution)/shard_map/all_to_all | solution.py:212
  39.8 10.3 %collective-permute-start.4 = (f32[32,24,128]{2,1,0:T(8,128)S(1)}, f32[32,24,128]{2,1,0:T(8,128)S(1)}, u32[]{:S(2)}, u32[]{:S(2)}) collective-permute-start(f32[32,24,128]{2,1,0:T(8,128)S(1)} %get-tuple-element.38), channel_id=1, source_target_pairs={{0,64},{64,0},{128,192},{192,128},{1,65},{65,1},{129,193},{193,129... | collective-permute-start | bytes 1179656 | tf_op jit(solution)/shard_map/ppermute | solution.py:209
  39.9 11.5 %collective-permute-start.5 = (f32[32,24,128]{2,1,0:T(8,128)S(1)}, f32[32,24,128]{2,1,0:T(8,128)S(1)}, u32[]{:S(2)}, u32[]{:S(2)}) collective-permute-start(f32[32,24,128]{2,1,0:T(8,128)S(1)} %get-tuple-element.39), channel_id=1, source_target_pairs={{0,192},{64,128},{128,64},{192,0},{1,193},{65,129},{129,65},{193,1... | collective-permute-start | bytes 1179656 | tf_op jit(solution)/shard_map/ppermute | solution.py:209
  43.9 16.0 %collective-permute-start.8 = (f32[32,24,128]{2,1,0:T(8,128)S(1)}, f32[32,24,128]{2,1,0:T(8,128)S(1)}, u32[]{:S(2)}, u32[]{:S(2)}) collective-permute-start(f32[32,24,128]{2,1,0:T(8,128)S(1)} %get-tuple-element.44), channel_id=1, source_target_pairs={{0,192},{64,128},{128,64},{192,0},{1,193},{65,129},{129,65},{193,1... | collective-permute-start | bytes 1179656 | tf_op jit(solution)/shard_map/ppermute | solution.py:209
  44.8 15.0 %collective-permute-start.9 = (f32[32,24,128]{2,1,0:T(8,128)S(1)}, f32[32,24,128]{2,1,0:T(8,128)S(1)}, u32[]{:S(2)}, u32[]{:S(2)}) collective-permute-start(f32[32,24,128]{2,1,0:T(8,128)S(1)} %get-tuple-element.45), channel_id=1, source_target_pairs={{0,64},{64,0},{128,192},{192,128},{1,65},{65,1},{129,193},{193,129... | collective-permute-start | bytes 1179656 | tf_op jit(solution)/shard_map/ppermute | solution.py:209
  60.9 34.2 %all-to-all-start.1 = ((f32[64,24,128]{2,1,0:T(8,128)}), f32[64,24,128]{2,1,0:T(8,128)S(1)}, u32[]{:S(2)}, u32[]{:S(2)}) async-start(f32[64,24,128]{2,1,0:T(8,128)} %shard_map.93), calls=%async_computation.1 | async-start | bytes 1572864 | tf_op jit(solution)/shard_map/all_to_all | solution.py:212

commit v5 on v4

--- a/solution.py
+++ b/solution.py
@@ -53,28 +53,22 @@
     low_out[...] = low_own[...] + low_in[...]
 
 
-def sum_kernel(top_own, low_own, top_near, low_near, top_far, low_far, out):
-    half = top_far.shape[0]
-    out[0:half] = top_own[...] + top_near[...] + top_far[...]
-    out[half:] = low_own[...] + low_near[...] + low_far[...]
-
-
 def first_add_kernel(top_own, low_own, top_in, low_in, top_out, low_out):
     top_out[...] = top_own[...] + top_in[1]
     low_out[...] = low_own[...] + low_in[1]
 
 
-def first_sum_kernel(top_own, low_own, top_near, low_near, top_far, low_far, named, out):
-    half, size = top_far.shape[:2]
-    pitch = out.shape[0] // (2 * half)
-    out[...] = jnp.zeros_like(out)
-    for o in range(half):
-        out[o * pitch : o * pitch + size] = top_own[o] + top_near[0, o] + top_far[o]
-        at = (half + o) * pitch
-        out[at : at + size] = low_own[o] + low_near[0, o] + low_far[o]
-    for o in range(2 * half):
-        at = o * pitch + size
-        out[at : at + 1] = named[o : o + 1]
+def first_sum_kernel(top_own, low_own, top_near, low_near, top_far, low_far, out):
+    half = top_far.shape[0]
+    out[0:half] = top_own[...] + top_near[0] + top_far[...]
+    out[half:] = low_own[...] + low_near[0] + low_far[...]
+
+
+def join_kernel(top_own, low_own, top_near, low_near, top_far, low_far, before, out):
+    half, done = top_far.shape[0], before.shape[1]
+    out[:, 0:done] = before[...]
+    out[0:half, done:] = top_own[...] + top_near[...] + top_far[...]
+    out[half:, done:] = low_own[...] + low_near[...] + low_far[...]
 
 
 def pair_rows(t):
@@ -112,14 +106,9 @@
     lax.fori_loop(0, target.shape[0] // (2 * slots), sources, 0)
 
 
-def first_kernel(slots, width, pitch, target, rows, dense, other):
-    scatter_rows(slots, 0, width, pitch, target, rows, dense, other)
+def scatter_kernel(slots, target, rows, count, dense, message, other):
+    scatter_rows(slots, 0, slots, slots, target, rows, dense, other)
     dense[...] += other[...]
-
-
-def last_kernel(slots, first, width, target, rows, before, count, dense, message, other):
-    scatter_rows(slots, first, width, width, target, rows, dense, other)
-    dense[...] += other[...] + before[...]
     values = dense[0 : dense.shape[0] - 8]
     square = jnp.sum(jnp.sum(values * values, axis=0, keepdims=True), axis=1, keepdims=True)
     touched = jnp.sum(count[...], axis=1, keepdims=True)
@@ -182,7 +171,9 @@
     counts = lax.dynamic_index_in_dim(block_counts[0], member, 0, keepdims=False)
     valid = jnp.arange(slots, dtype=jnp.int32)[None, :] < counts[:, None]
     named = jnp.where(valid, ids, blocks).astype(f32)
-    named = jnp.pad(named, ((0, 0), (0, lanes - slots)))
+    named = jnp.pad(named, ((0, 0), (0, lanes - slots))).reshape(owners, 1, lanes)
+    named = lax.all_to_all(named, OWN, split_axis=0, concat_axis=0, tiled=True)
+    target = named.reshape(owners, lanes)[:, :slots].astype(jnp.int32).reshape(-1)
 
     flip, mirror = member ^ 1, 3 - member
     order = jnp.stack([flip, mirror, mirror ^ 1, member])
@@ -207,9 +198,6 @@
 
     def permuted(top, low, top_pairs, low_pairs):
         return lax.ppermute(top, "grp", top_pairs), lax.ppermute(low, "grp", low_pairs)
-
-    def exchange(share):
-        return lax.all_to_all(share, OWN, split_axis=0, concat_axis=0, tiled=True)
 
     staged = ((1, 0), (0, 1), (3, 0), (3, 1))
 
@@ -224,13 +212,8 @@
     ins = (kept[0], kept[1], *near)
     top, low = call(first_add_kernel, (piece, piece), ins)
     far = permuted(top, low, mirrors, flips)
-    pitch = size + 2
-    ins = (kept[2], kept[3], *near, *far, named)
-    share = call(first_sum_kernel, shape(owners * pitch, lanes), ins, True)
-    share = exchange(share.reshape(owners, 1, pitch * lanes))
-    named = share[:, 0, size * lanes : size * lanes + slots]
-    target = named.astype(jnp.int32).reshape(-1)
-    shares = [share.reshape(owners * pitch, lanes)]
+    ins = (kept[2], kept[3], *near, *far)
+    before = call(first_sum_kernel, shape(owners, size, lanes), ins, True)
 
     span = spans[1]
     size = span[1] - span[0]
@@ -244,27 +227,23 @@
     ins = (kept[0], kept[1], *late)
     top, low = call(add_kernel, (piece, piece), ins)
     far = permuted(top, low, mirrors, flips)
-    ins = (kept[2], kept[3], *near, *far)
-    share = call(sum_kernel, shape(owners, size, lanes), ins, True)
-    share = exchange(share)
-    shares.append(share.reshape(owners * size, lanes))
+    ins = (kept[2], kept[3], *near, *far, before)
+    share = call(join_kernel, shape(owners, span[1], lanes), ins, True)
+    share = lax.all_to_all(share, OWN, split_axis=0, concat_axis=0, tiled=True)
+    share = share.reshape(owners * slots * features, lanes)
 
     rows = blocks * features
     table = shape(rows + 8, lanes)
     mask, count = kernel_call(
         functools.partial(mark_kernel, slots), (table, shape(1, lanes)), [SMEM], (VMEM, VMEM)
     )(target)
-    spare = [pltpu.VMEM(table.shape, f32)]
-    before = kernel_call(
-        functools.partial(first_kernel, slots, CHUNKS[0], pitch // features), table, [SMEM, VMEM], VMEM, spare
-    )(target, shares[0])
     dense, message = kernel_call(
-        functools.partial(last_kernel, slots, CHUNKS[0], CHUNKS[1]),
+        functools.partial(scatter_kernel, slots),
         (table, shape(devices, lanes)),
-        [SMEM] + [VMEM] * 3,
+        [SMEM, VMEM, VMEM],
         (VMEM, VMEM),
-        spare,
-    )(target, shares[1], before, count)
+        [pltpu.VMEM(table.shape, f32)],
+    )(target, share, count)
     messages = lax.all_to_all(
         message.reshape(devices, 1, lanes), GRP_OWN, split_axis=0, concat_axis=0, tiled=True
     ).reshape(devices, lanes)

time: 122 us -> 124 us (1.016)
  waiting for transfers between devices: 43.7 us -> 35.8 us
  local copies, waits for them, and re-layouts: 0.87 us -> 6.17 us
  blocking collectives: 20.5 us -> 22.4 us
  Pallas kernels: 20.6 us -> 22.4 us
    ppermute x5, waiting for transfers between devices: 23.2 us -> 2.39 us  [permuted(): lax.ppermute(top, 'grp', top_pairs)]
    all_to_all x2, waiting for transfers between devices: 19.2 us -> 33.4 us  [the longest x1 26.2 us: step(): share = lax.all_to_all(share, OWN, split_axis=0, concat_axis=0, tiled=True)]
    unnamed x2 -> x20, local copies, waits for them, and re-layouts: 0.01 us -> 5.4 us
    all_to_all x1, blocking collectives: 20.5 us -> 22.4 us  [step(): lax.all_to_all(message.reshape(devices, 1, lanes), GRP_OWN, split_axis=0,...]
    pallas_call x5, Pallas kernels: 9.38 us -> 11.1 us  [copied(): kernel_call(functools.partial(copies_kernel, plan), outs, [SMEM, ANY], (V...]
    ppermute x5, waiting for transfers between devices: 1.34 us -> 0.01 us  [permuted(): lax.ppermute(low, 'grp', low_pairs)]
    pallas_call x2 -> x1, Pallas kernels: 3.74 us -> 2.87 us  [step(): kernel_call(functools.partial(scatter_kernel, slots), (table, shape(devic...]
  transfers between devices with their start and end apart: 12 -> 12, of which waited for: 5 -> 3; matrix products, arithmetic and copies ran while one was open for 1% -> 1% of each run, Pallas kernels for 11% -> 11%
where the time goes in v5:
time: 124 us
  waiting for transfers between devices  35.8 us (29%)
  starting transfers between devices  35.1 us (28%)
  Pallas kernels  22.4 us (18%)
  blocking collectives  22.4 us (18%)
  local copies, waits for them, and re-layouts  6.17 us (5%)
    all_to_all x1, waiting for transfers between devices, step(): share = lax.all_to_all(share, OWN, split_axis=0, concat_axis=0, tiled=True)  26.2 us
    all_to_all x1, blocking collectives, step(): lax.all_to_all(message.reshape(devices, 1, lanes), GRP_OWN, split_axis=0,...  22.4 us
    all_to_all x1, starting transfers between devices, step(): named = lax.all_to_all(named, OWN, split_axis=0, concat_axis=0, tiled=True)  19.1 us
    pallas_call x5, Pallas kernels, copied(): kernel_call(functools.partial(copies_kernel, plan), outs, [SMEM, ANY], (V...  11.1 us
    all_to_all x1, waiting for transfers between devices, step(): named = lax.all_to_all(named, OWN, split_axis=0, concat_axis=0, tiled=True)  7.2 us
    ppermute x5, starting transfers between devices, permuted(): lax.ppermute(top, 'grp', top_pairs)  6.04 us
    unnamed x20, local copies, waits for them, and re-layouts  5.4 us
    ppermute x5, starting transfers between devices, permuted(): lax.ppermute(low, 'grp', low_pairs)  5.22 us
  transfers between devices with their start and end apart: 12, of which 3 were waited for; matrix products, arithmetic and copies ran while one was open for 1% of the time, Pallas kernels for 11%

profile of v5, /device:TPU:1, one launch (start us, length us, event | category | flops | bytes accessed | tf_op | source)
XLA Modules:
  0.0 123.5 jit_solution(16977717163084461253)
XLA Ops:
  0.6 0.0 copy-start
  0.7 0.1 pad_add_fusion.order
  0.7 2.6 %shard_map.87 = (f32[32,24,128]{2,1,0:T(8,128)}, f32[32,24,128]{2,1,0:T(8,128)}) custom-call(s32[4]{0:T(128)S(1)} %pad_add_fusion.order, f32[4,64,32,128]{3,2,1,0:T(8,128)} %bitcast.28), custom_call_target="tpu_custom_call" | custom-call | flops 262144 | bytes 1048576 | tf_op jit(solution)/shard_map/pallas_call | solution.py:184
  3.3 2.1 %collective-permute-start.2 = (f32[32,24,128]{2,1,0:T(8,128)}, f32[32,24,128]{2,1,0:T(8,128)S(1)}, u32[]{:S(2)}, u32[]{:S(2)}) collective-permute-start(f32[32,24,128]{2,1,0:T(8,128)} %get-tuple-element.34), channel_id=1, source_target_pairs={{0,64},{64,0},{128,192},{192,128},{1,65},{65,1},{129,193},{193,129... | collective-permute-start | bytes 1179656 | tf_op jit(solution)/shard_map/ppermute | solution.py:200
  5.4 1.8 %collective-permute-start.3 = (f32[32,24,128]{2,1,0:T(8,128)}, f32[32,24,128]{2,1,0:T(8,128)S(1)}, u32[]{:S(2)}, u32[]{:S(2)}) collective-permute-start(f32[32,24,128]{2,1,0:T(8,128)} %get-tuple-element.35), channel_id=1, source_target_pairs={{0,192},{64,128},{128,64},{192,0},{1,193},{65,129},{129,65},{193,1... | collective-permute-start | bytes 1179656 | tf_op jit(solution)/shard_map/ppermute | solution.py:200
  7.3 2.5 %shard_map.90 = (f32[2,32,8,128]{3,2,1,0:T(8,128)}, f32[2,32,8,128]{3,2,1,0:T(8,128)}) custom-call(s32[4]{0:T(128)S(1)} %pad_add_fusion.order, f32[4,64,32,128]{3,2,1,0:T(8,128)} %bitcast.29), custom_call_target="tpu_custom_call" | custom-call | flops 262144 | bytes 2097152 | tf_op jit(solution)/shard_map/pallas_call | solution.py:184
  9.8 0.4 collective-permute-start.6
  10.2 0.6 collective-permute-start.7
  10.8 2.4 %shard_map.86 = (f32[32,24,128]{2,1,0:T(8,128)}, f32[32,24,128]{2,1,0:T(8,128)S(1)}) custom-call(s32[4]{0:T(128)S(1)} %pad_add_fusion.order, f32[4,64,32,128]{3,2,1,0:T(8,128)} %bitcast.30), custom_call_target="tpu_custom_call" | custom-call | flops 262144 | bytes 1048576 | tf_op jit(solution)/shard_map/pallas_call | solution.py:184
  13.2 0.0 copy-start.9
  13.2 0.8 collective-permute-start
  14.1 1.7 %shard_map.89 = (f32[32,8,128]{2,1,0:T(8,128)S(1)}, f32[32,8,128]{2,1,0:T(8,128)S(1)}, f32[32,8,128]{2,1,0:T(8,128)S(1)}, f32[32,8,128]{2,1,0:T(8,128)S(1)}) custom-call(s32[4]{0:T(128)S(1)} %pad_add_fusion.order, f32[4,64,32,128]{3,2,1,0:T(8,128)} %bitcast.31), custom_call_target="tpu_custom_call" | custom-call | flops 262144 | bytes 2097152 | tf_op jit(solution)/shard_map/pallas_call | solution.py:184
  15.8 0.0 copy-done.9
  15.8 0.0 copy-start.5
  15.8 0.6 copy-done.5
  16.4 0.0 copy-start.7
  16.4 0.6 copy-done.7
  17.1 1.9 %shard_map.85 = (f32[32,24,128]{2,1,0:T(8,128)S(1)}, f32[32,24,128]{2,1,0:T(8,128)S(1)}, f32[32,24,128]{2,1,0:T(8,128)S(1)}, f32[32,24,128]{2,1,0:T(8,128)S(1)}) custom-call(s32[4]{0:T(128)S(1)} %pad_add_fusion.order, f32[4,64,32,128]{3,2,1,0:T(8,128)} %bitcast.32), custom_call_target="tpu_custom_call" | custom-call | flops 262144 | bytes 2097152 | tf_op jit(solution)/shard_map/pallas_call | solution.py:184
  19.0 0.0 copy-start.1
  19.0 0.7 copy-done.1
  19.8 0.0 copy-done
  19.8 0.0 copy-start.2
  19.8 0.0 collective-permute-done.6.top_in.top_near
  19.8 2.8 %collective-permute-start.1 = (f32[32,24,128]{2,1,0:T(8,128)}, f32[32,24,128]{2,1,0:T(8,128)S(1)}, u32[]{:S(2)}, u32[]{:S(2)}) collective-permute-start(f32[32,24,128]{2,1,0:T(8,128)} %copy-done.9), channel_id=1, source_target_pairs={{0,192},{64,128},{128,64},{192,0},{1,193},{65,129},{129,65},{193,1... | collective-permute-start | bytes 1179656 | tf_op jit(solution)/shard_map/ppermute | solution.py:200
  22.5 0.0 collective-permute-done.7.low_in.low_near
  22.5 0.0 copy-start.6
  22.5 0.9 copy-done.6
  23.4 0.0 copy-start.8
  23.4 0.9 copy-done.8
  24.3 0.7 shard_map.91
  25.0 1.5 %collective-permute-start.8 = (f32[32,8,128]{2,1,0:T(8,128)S(1)}, f32[32,8,128]{2,1,0:T(8,128)S(1)}, u32[]{:S(2)}, u32[]{:S(2)}) collective-permute-start(f32[32,8,128]{2,1,0:T(8,128)S(1)} %get-tuple-element.44), channel_id=1, source_target_pairs={{0,192},{64,128},{128,64},{192,0},{1,193},{65,129},{129,65},{193,1... | collective-permute-start | bytes 393224 | tf_op jit(solution)/shard_map/ppermute | solution.py:200
  26.5 0.0 collective-permute-done.2.top_in
  26.5 0.0 collective-permute-done.3.low_in
  26.5 0.0 copy-done.2
  26.5 1.0 shard_map.88
  27.5 1.2 collective-permute-start.4
  28.7 0.0 collective-permute-start.5
  28.7 0.7 fusion
  29.4 2.4 %collective-permute-done.8.top_far = f32[32,8,128]{2,1,0:T(8,128)S(1)} collective-permute-done((f32[32,8,128]{2,1,0:T(8,128)S(1)}, f32[32,8,128]{2,1,0:T(8,128)S(1)}, u32[]{:S(2)}, u32[]{:S(2)}) %collective-permute-start.8) | collective-permute-done | bytes 131104 | tf_op jit(solution)/shard_map/ppermute | solution.py:200
  31.7 0.0 copy-start.3
  31.8 0.7 copy-done.3
  32.4 0.0 collective-permute-start.9
  32.4 0.7 copy.10
  33.1 19.1 %all-to-all-start = ((f32[64,1,128]{2,1,0:T(1,128)}), f32[64,1,128]{2,1,0:T(1,128)S(1)}, u32[]{:S(2)}, u32[]{:S(2)}) async-start(f32[64,1,128]{2,1,0:T(1,128)} %copy.10), calls=%async_computation | async-start | bytes 65536 | tf_op jit(solution)/shard_map/all_to_all | solution.py:175
  52.2 0.0 collective-permute-done.9.low_far
  52.2 0.0 copy-start.4
  52.2 0.9 copy-done.4
  53.2 0.0 collective-permute-done.top_near
  53.2 0.0 collective-permute-done.1.low_near
  53.2 0.0 collective-permute-done.4.top_far
  53.2 0.0 collective-permute-done.5.low_far
  53.2 1.1 shard_map.93
  54.3 7.2 %all-to-all-done = f32[64,1,128]{2,1,0:T(1,128)S(1)} async-done(((f32[64,1,128]{2,1,0:T(1,128)}), f32[64,1,128]{2,1,0:T(1,128)S(1)}, u32[]{:S(2)}, u32[]{:S(2)}) %all-to-all-start) | async-done | bytes 32800 | tf_op jit(solution)/shard_map/all_to_all | solution.py:175
  61.5 4.7 %all-to-all-start.1 = ((f32[64,32,128]{2,1,0:T(8,128)}), f32[64,32,128]{2,1,0:T(8,128)S(1)}, u32[]{:S(2)}, u32[]{:S(2)}) async-start(f32[64,32,128]{2,1,0:T(8,128)} %shard_map.93), calls=%async_computation.1 | async-start | bytes 2097152 | tf_op jit(solution)/shard_map/all_to_all | solution.py:232
  66.3 0.1 reshape.53.target
  66.4 2.3 %shard_map.94 = (f32[2056,128]{1,0:T(8,128)S(1)}, f32[1,128]{1,0:T(1,128)S(1)}) custom-call(s32[1024]{0:T(1024)S(1)} %reshape.53.target), custom_call_target="tpu_custom_call" | custom-call | flops 262144 | bytes 1048576 | tf_op jit(solution)/shard_map/pallas_call | solution.py:237
  68.6 26.2 %all-to-all-done.1 = f32[64,32,128]{2,1,0:T(8,128)S(1)} async-done(((f32[64,32,128]{2,1,0:T(8,128)}), f32[64,32,128]{2,1,0:T(8,128)S(1)}, u32[]{:S(2)}, u32[]{:S(2)}) %all-to-all-start.1) | async-done | bytes 1048608 | tf_op jit(solution)/shard_map/all_to_all | solution.py:232
  94.8 2.9 %shard_map.95 = (f32[2056,128]{1,0:T(8,128)S(1)}, f32[256,128]{1,0:T(8,128)S(1)}) custom-call(s32[1024]{0:T(1024)S(1)} %reshape.53.target, f32[2048,128]{1,0:T(8,128)S(1)} %bitcast.25, f32[1,128]{1,0:T(1,128)S(1)} %get-tuple-element.46.count), custom_call_target="tpu_custom_call" | custom-call | flops 262144 | bytes 1048576 | tf_op jit(solution)/shard_map/pallas_call | solution.py:240
  97.7 22.4 %all_to_all.15 = f32[256,1,128]{2,1,0:T(1,128)S(1)} all-to-all(f32[256,1,128]{2,1,0:T(1,128)S(1)} %bitcast.27), channel_id=1, replica_groups=mesh['grp'=4,'own_0'=4,'own_1'=8,'own_2'=2] {'grp','own_0','own_1','own_2'}, dimensions={0} | all-to-all | bytes 262144 | tf_op jit(solution)/shard_map/all_to_all | solution.py:247
  120.2 3.4 %shard_map.96 = (f32[2048,128]{1,0:T(8,128)}, f32[2048,128]{1,0:T(8,128)}, f32[2048,128]{1,0:T(8,128)}) custom-call(f32[256,128]{1,0:T(8,128)S(1)} %bitcast.26, f32[2056,128]{1,0:T(8,128)S(1)} %get-tuple-element.48.dense, f32[2056,128]{1,0:T(8,128)S(1)} %get-tuple-element.49.mask, f32[2048,128]{1,0:T(8,128)} %bitcast.33, f32[2048,128]{1,0:T(8,128)} %bitcast.34, ...), custom_call_target="tpu_custom_call" | custom-call | flops 262144 | bytes 1048576 | tf_op jit(solution)/shard_map/pallas_call | solution.py:252
  (4 shorter events, 0.1 us)
Async XLA Ops:
  0.6 19.1 %copy-start = (s32[1,4,64]{2,1,0:T(4,128)S(1)}, s32[1,4,64]{2,1,0:T(4,128)}, u32[]{:S(2)}) copy-start(s32[1,4,64]{2,1,0:T(4,128)} %param.8) | copy-start | bytes 3076
  3.3 23.2 %collective-permute-start.2 = (f32[32,24,128]{2,1,0:T(8,128)}, f32[32,24,128]{2,1,0:T(8,128)S(1)}, u32[]{:S(2)}, u32[]{:S(2)}) collective-permute-start(f32[32,24,128]{2,1,0:T(8,128)} %get-tuple-element.34), channel_id=1, source_target_pairs={{0,64},{64,0},{128,192},{192,128},{1,65},{65,1},{129,193},{193,129... | collective-permute-start | bytes 1179656 | tf_op jit(solution)/shard_map/ppermute | solution.py:200
  5.4 21.1 %collective-permute-start.3 = (f32[32,24,128]{2,1,0:T(8,128)}, f32[32,24,128]{2,1,0:T(8,128)S(1)}, u32[]{:S(2)}, u32[]{:S(2)}) collective-permute-start(f32[32,24,128]{2,1,0:T(8,128)} %get-tuple-element.35), channel_id=1, source_target_pairs={{0,192},{64,128},{128,64},{192,0},{1,193},{65,129},{129,65},{193,1... | collective-permute-start | bytes 1179656 | tf_op jit(solution)/shard_map/ppermute | solution.py:200
  9.8 10.0 %collective-permute-start.6 = (f32[2,32,8,128]{3,2,1,0:T(8,128)}, f32[2,32,8,128]{3,2,1,0:T(8,128)S(1)}, u32[]{:S(2)}, u32[]{:S(2)}) collective-permute-start(f32[2,32,8,128]{3,2,1,0:T(8,128)} %get-tuple-element.40), channel_id=1, source_target_pairs={{0,64},{64,0},{128,192},{192,128},{1,65},{65,1},{129,193},{193,129... | collective-permute-start | bytes 786440 | tf_op jit(solution)/shard_map/ppermute | solution.py:200
  10.2 12.4 %collective-permute-start.7 = (f32[2,32,8,128]{3,2,1,0:T(8,128)}, f32[2,32,8,128]{3,2,1,0:T(8,128)S(1)}, u32[]{:S(2)}, u32[]{:S(2)}) collective-permute-start(f32[2,32,8,128]{3,2,1,0:T(8,128)} %get-tuple-element.41), channel_id=1, source_target_pairs={{0,192},{64,128},{128,64},{192,0},{1,193},{65,129},{129,65},{193,1... | collective-permute-start | bytes 786440 | tf_op jit(solution)/shard_map/ppermute | solution.py:200
  13.2 2.5 %copy-start.9 = (f32[32,24,128]{2,1,0:T(8,128)}, f32[32,24,128]{2,1,0:T(8,128)S(1)}, u32[]{:S(2)}) copy-start(f32[32,24,128]{2,1,0:T(8,128)S(1)} %get-tuple-element.31) | copy-start | bytes 1179652
  13.2 39.9 %collective-permute-start = (f32[32,24,128]{2,1,0:T(8,128)}, f32[32,24,128]{2,1,0:T(8,128)S(1)}, u32[]{:S(2)}, u32[]{:S(2)}) collective-permute-start(f32[32,24,128]{2,1,0:T(8,128)} %get-tuple-element.30), channel_id=1, source_target_pairs={{0,64},{64,0},{128,192},{192,128},{1,65},{65,1},{129,193},{193,129... | collective-permute-start | bytes 1179656 | tf_op jit(solution)/shard_map/ppermute | solution.py:200
  15.8 0.6 copy-start.5
  16.4 0.6 copy-start.7
  19.0 0.7 copy-start.1
  19.8 6.7 %copy-start.2 = (f32[32,24,128]{2,1,0:T(8,128)S(1)}, f32[32,24,128]{2,1,0:T(8,128)}, u32[]{:S(2)}) copy-start(f32[32,24,128]{2,1,0:T(8,128)} %copy-done.1) | copy-start | bytes 1179652
  19.8 33.4 %collective-permute-start.1 = (f32[32,24,128]{2,1,0:T(8,128)}, f32[32,24,128]{2,1,0:T(8,128)S(1)}, u32[]{:S(2)}, u32[]{:S(2)}) collective-permute-start(f32[32,24,128]{2,1,0:T(8,128)} %copy-done.9), channel_id=1, source_target_pairs={{0,192},{64,128},{128,64},{192,0},{1,193},{65,129},{129,65},{193,1... | collective-permute-start | bytes 1179656 | tf_op jit(solution)/shard_map/ppermute | solution.py:200
  22.5 0.9 copy-start.6
  23.4 0.9 copy-start.8
  25.0 6.7 %collective-permute-start.8 = (f32[32,8,128]{2,1,0:T(8,128)S(1)}, f32[32,8,128]{2,1,0:T(8,128)S(1)}, u32[]{:S(2)}, u32[]{:S(2)}) collective-permute-start(f32[32,8,128]{2,1,0:T(8,128)S(1)} %get-tuple-element.44), channel_id=1, source_target_pairs={{0,192},{64,128},{128,64},{192,0},{1,193},{65,129},{129,65},{193,1... | collective-permute-start | bytes 393224 | tf_op jit(solution)/shard_map/ppermute | solution.py:200
  27.5 25.7 %collective-permute-start.4 = (f32[32,24,128]{2,1,0:T(8,128)}, f32[32,24,128]{2,1,0:T(8,128)S(1)}, u32[]{:S(2)}, u32[]{:S(2)}) collective-permute-start(f32[32,24,128]{2,1,0:T(8,128)} %get-tuple-element.36), channel_id=1, source_target_pairs={{0,192},{64,128},{128,64},{192,0},{1,193},{65,129},{129,65},{193,1... | collective-permute-start | bytes 1179656 | tf_op jit(solution)/shard_map/ppermute | solution.py:200
  28.7 24.5 %collective-permute-start.5 = (f32[32,24,128]{2,1,0:T(8,128)}, f32[32,24,128]{2,1,0:T(8,128)S(1)}, u32[]{:S(2)}, u32[]{:S(2)}) collective-permute-start(f32[32,24,128]{2,1,0:T(8,128)} %get-tuple-element.37), channel_id=1, source_target_pairs={{0,64},{64,0},{128,192},{192,128},{1,65},{65,1},{129,193},{193,129... | collective-permute-start | bytes 1179656 | tf_op jit(solution)/shard_map/ppermute | solution.py:200
  31.7 0.7 copy-start.3
  32.4 19.8 %collective-permute-start.9 = (f32[32,8,128]{2,1,0:T(8,128)}, f32[32,8,128]{2,1,0:T(8,128)S(1)}, u32[]{:S(2)}, u32[]{:S(2)}) collective-permute-start(f32[32,8,128]{2,1,0:T(8,128)} %get-tuple-element.45), channel_id=1, source_target_pairs={{0,64},{64,0},{128,192},{192,128},{1,65},{65,1},{129,193},{193,129... | collective-permute-start | bytes 393224 | tf_op jit(solution)/shard_map/ppermute | solution.py:200
  33.1 28.4 %all-to-all-start = ((f32[64,1,128]{2,1,0:T(1,128)}), f32[64,1,128]{2,1,0:T(1,128)S(1)}, u32[]{:S(2)}, u32[]{:S(2)}) async-start(f32[64,1,128]{2,1,0:T(1,128)} %copy.10), calls=%async_computation | async-start | bytes 65536 | tf_op jit(solution)/shard_map/all_to_all | solution.py:175
  52.2 0.9 copy-start.4
  61.5 33.3 %all-to-all-start.1 = ((f32[64,32,128]{2,1,0:T(8,128)}), f32[64,32,128]{2,1,0:T(8,128)S(1)}, u32[]{:S(2)}, u32[]{:S(2)}) async-start(f32[64,32,128]{2,1,0:T(8,128)} %shard_map.93), calls=%async_computation.1 | async-start | bytes 2097152 | tf_op jit(solution)/shard_map/all_to_all | solution.py:232

commit v6 on v4

--- a/solution.py
+++ b/solution.py
@@ -12,7 +12,7 @@
 OWN = ("own_0", "own_1", "own_2")
 GRP_OWN = ("grp", "own_0", "own_1", "own_2")
 CHUNKS = (4, 12)
-STEPS = 4
+STEPS = 8
 f32 = jnp.float32
 ANY = pl.BlockSpec(memory_space=pl.ANY)
 VMEM = pl.BlockSpec(memory_space=pltpu.VMEM)
@@ -239,12 +239,11 @@
     late = permuted(*sent, flips, mirrors)
     sent = copied((piece,) * 2, ((0, None, 0, 0, span), (1, None, 1, 1, span)))
     near = permuted(*sent, flips, mirrors)
-    plan = tuple((n, None, which, part, span) for n, (which, part) in enumerate(staged))
-    kept = copied((piece,) * 4, plan)
-    ins = (kept[0], kept[1], *late)
-    top, low = call(add_kernel, (piece, piece), ins)
+    kept = copied((piece,) * 2, ((0, None, 1, 0, span), (1, None, 0, 1, span)))
+    top, low = call(add_kernel, (piece, piece), (*kept, *late))
     far = permuted(top, low, mirrors, flips)
-    ins = (kept[2], kept[3], *near, *far)
+    kept = copied((piece,) * 2, ((0, None, 3, 0, span), (1, None, 3, 1, span)))
+    ins = (*kept, *near, *far)
     share = call(sum_kernel, shape(owners, size, lanes), ins, True)
     share = exchange(share)
     shares.append(share.reshape(owners * size, lanes))

time: 122 us -> 122 us (level)
  waiting for transfers between devices: 43.7 us -> 42.3 us
    ppermute x5, waiting for transfers between devices: 23.2 us -> 21.1 us  [permuted(): lax.ppermute(top, 'grp', top_pairs)]
    pallas_call x5 -> x6, Pallas kernels: 9.38 us -> 10.1 us  [copied(): kernel_call(functools.partial(copies_kernel, plan), outs, [SMEM, ANY], (V...]
  transfers between devices with their start and end apart: 12 -> 12, of which waited for: 5 -> 6; matrix products, arithmetic and copies ran while one was open for 1% -> 1% of each run, Pallas kernels for 11% -> 11%
where the time goes in v6:
time: 122 us; the launch traced here: 121 us
  waiting for transfers between devices  42.3 us (35%)
  starting transfers between devices  35.3 us (29%)
  Pallas kernels  21.2 us (17%)
  blocking collectives  20.5 us (17%)
    all_to_all x2, starting transfers between devices, exchange(): return lax.all_to_all(share, OWN, split_axis=0, concat_axis=0, tiled=True)  25 us
    ppermute x5, waiting for transfers between devices, permuted(): lax.ppermute(top, 'grp', top_pairs)  21.1 us
    all_to_all x1, blocking collectives, step(): lax.all_to_all(message.reshape(devices, 1, lanes), GRP_OWN, split_axis=0,...  20.5 us
    all_to_all x2, waiting for transfers between devices, exchange(): return lax.all_to_all(share, OWN, split_axis=0, concat_axis=0, tiled=True)  19.2 us
    pallas_call x6, Pallas kernels, copied(): kernel_call(functools.partial(copies_kernel, plan), outs, [SMEM, ANY], (V...  10.1 us
    ppermute x5, starting transfers between devices, permuted(): lax.ppermute(top, 'grp', top_pairs)  5.78 us
    ppermute x5, starting transfers between devices, permuted(): lax.ppermute(low, 'grp', low_pairs)  4.52 us
    pallas_call x1, Pallas kernels, step(): kernel_call(update_kernel, (flat,) * 3, [VMEM] * 3 + [ANY] * 3, (ANY,) *...  3.26 us
  transfers between devices with their start and end apart: 12, of which 6 were waited for; matrix products, arithmetic and copies ran while one was open for 1% of the time, Pallas kernels for 11%

profile of v6, /device:TPU:1, one launch (start us, length us, event | category | flops | bytes accessed | tf_op | source)
XLA Modules:
  0.0 121.3 jit_solution(6578378179112477076)
XLA Ops:
  0.6 0.0 copy-start
  0.7 0.1 pad_add_fusion.order
  0.7 1.7 %shard_map.86 = (f32[2,32,8,128]{3,2,1,0:T(8,128)S(1)}, f32[2,32,8,128]{3,2,1,0:T(8,128)S(1)}) custom-call(s32[4]{0:T(128)S(1)} %pad_add_fusion.order, f32[4,64,32,128]{3,2,1,0:T(8,128)} %bitcast.28), custom_call_target="tpu_custom_call" | custom-call | flops 262144 | bytes 2097152 | tf_op jit(solution)/shard_map/pallas_call | solution.py:193
  2.4 2.1 %collective-permute-start = (f32[2,32,8,128]{3,2,1,0:T(8,128)S(1)}, f32[2,32,8,128]{3,2,1,0:T(8,128)S(1)}, u32[]{:S(2)}, u32[]{:S(2)}) collective-permute-start(f32[2,32,8,128]{3,2,1,0:T(8,128)S(1)} %get-tuple-element.30), channel_id=1, source_target_pairs={{0,64},{64,0},{128,192},{192,128},{1,65},{65,1},{129,193},{193,129... | collective-permute-start | bytes 786440 | tf_op jit(solution)/shard_map/ppermute | solution.py:209
  4.5 1.8 %collective-permute-start.1 = (f32[2,32,8,128]{3,2,1,0:T(8,128)S(1)}, f32[2,32,8,128]{3,2,1,0:T(8,128)S(1)}, u32[]{:S(2)}, u32[]{:S(2)}) collective-permute-start(f32[2,32,8,128]{3,2,1,0:T(8,128)S(1)} %get-tuple-element.31), channel_id=1, source_target_pairs={{0,192},{64,128},{128,64},{192,0},{1,193},{65,129},{129,65},{193,1... | collective-permute-start | bytes 786440 | tf_op jit(solution)/shard_map/ppermute | solution.py:209
  6.3 1.7 %shard_map.92 = (f32[32,24,128]{2,1,0:T(8,128)S(1)}, f32[32,24,128]{2,1,0:T(8,128)S(1)}) custom-call(s32[4]{0:T(128)S(1)} %pad_add_fusion.order, f32[4,64,32,128]{3,2,1,0:T(8,128)} %bitcast.29), custom_call_target="tpu_custom_call" | custom-call | flops 262144 | bytes 1048576 | tf_op jit(solution)/shard_map/pallas_call | solution.py:193
  8.0 0.4 collective-permute-start.6
  8.4 0.6 collective-permute-start.7
  9.1 1.7 %shard_map.85 = (f32[32,8,128]{2,1,0:T(8,128)S(1)}, f32[32,8,128]{2,1,0:T(8,128)S(1)}, f32[32,8,128]{2,1,0:T(8,128)S(1)}, f32[32,8,128]{2,1,0:T(8,128)S(1)}) custom-call(s32[4]{0:T(128)S(1)} %pad_add_fusion.order, f32[4,64,32,128]{3,2,1,0:T(8,128)} %bitcast.30), custom_call_target="tpu_custom_call" | custom-call | flops 262144 | bytes 2097152 | tf_op jit(solution)/shard_map/pallas_call | solution.py:193
  10.8 0.0 copy-done
  10.8 0.1 copy.11
  10.9 0.7 dynamic-slice_bitcast_fusion
  11.6 0.0 collective-permute-done.top_in.top_near
  11.6 0.8 collective-permute-done.1.low_in.low_near
  12.4 2.2 %collective-permute-start.2 = (f32[32,8,128]{2,1,0:T(8,128)S(1)}, f32[32,8,128]{2,1,0:T(8,128)S(1)}, u32[]{:S(2)}, u32[]{:S(2)}) collective-permute-start(f32[32,8,128]{2,1,0:T(8,128)S(1)} %get-tuple-element.34), channel_id=1, source_target_pairs={{0,192},{64,128},{128,64},{192,0},{1,193},{65,129},{129,65},{193,1... | collective-permute-start | bytes 393224 | tf_op jit(solution)/shard_map/ppermute | solution.py:209
  14.6 0.0 collective-permute-start.3
  14.6 0.1 fusion.1
  14.7 8.9 %collective-permute-done.2.top_far = f32[32,8,128]{2,1,0:T(8,128)S(1)} collective-permute-done((f32[32,8,128]{2,1,0:T(8,128)S(1)}, f32[32,8,128]{2,1,0:T(8,128)S(1)}, u32[]{:S(2)}, u32[]{:S(2)}) %collective-permute-start.2) | collective-permute-done | bytes 131104 | tf_op jit(solution)/shard_map/ppermute | solution.py:209
  23.6 0.0 collective-permute-done.3.low_far
  23.6 0.8 shard_map.88
  24.4 13.8 %all-to-all-start = ((f32[64,1,1280]{2,1,0:T(1,128)}), f32[64,1,1280]{2,1,0:T(1,128)S(1)}, u32[]{:S(2)}, u32[]{:S(2)}) async-start(f32[64,1,1280]{2,1,0:T(1,128)} %bitcast.7), calls=%async_computation | async-start | bytes 655360 | tf_op jit(solution)/shard_map/all_to_all | solution.py:212
  38.2 1.7 %shard_map.90 = (f32[32,24,128]{2,1,0:T(8,128)S(1)}, f32[32,24,128]{2,1,0:T(8,128)S(1)}) custom-call(s32[4]{0:T(128)S(1)} %pad_add_fusion.order, f32[4,64,32,128]{3,2,1,0:T(8,128)} %bitcast.31), custom_call_target="tpu_custom_call" | custom-call | flops 262144 | bytes 1048576 | tf_op jit(solution)/shard_map/pallas_call | solution.py:193
  39.8 0.1 collective-permute-start.4
  39.9 1.9 %collective-permute-start.5 = (f32[32,24,128]{2,1,0:T(8,128)S(1)}, f32[32,24,128]{2,1,0:T(8,128)S(1)}, u32[]{:S(2)}, u32[]{:S(2)}) collective-permute-start(f32[32,24,128]{2,1,0:T(8,128)S(1)} %get-tuple-element.39), channel_id=1, source_target_pairs={{0,192},{64,128},{128,64},{192,0},{1,193},{65,129},{129,65},{193,1... | collective-permute-start | bytes 1179656 | tf_op jit(solution)/shard_map/ppermute | solution.py:209
  41.8 1.7 %shard_map.91 = (f32[32,24,128]{2,1,0:T(8,128)S(1)}, f32[32,24,128]{2,1,0:T(8,128)S(1)}) custom-call(s32[4]{0:T(128)S(1)} %pad_add_fusion.order, f32[4,64,32,128]{3,2,1,0:T(8,128)} %bitcast.32), custom_call_target="tpu_custom_call" | custom-call | flops 262144 | bytes 1048576 | tf_op jit(solution)/shard_map/pallas_call | solution.py:193
  43.5 0.0 collective-permute-done.6.top_in
  43.5 0.0 collective-permute-done.7.low_in
  43.5 0.1 shard_map.93
  43.6 0.9 collective-permute-start.8
  44.6 0.2 collective-permute-start.9
  44.7 1.7 %shard_map.89 = (f32[32,24,128]{2,1,0:T(8,128)S(1)}, f32[32,24,128]{2,1,0:T(8,128)S(1)}) custom-call(s32[4]{0:T(128)S(1)} %pad_add_fusion.order, f32[4,64,32,128]{3,2,1,0:T(8,128)} %bitcast.33), custom_call_target="tpu_custom_call" | custom-call | flops 262144 | bytes 1048576 | tf_op jit(solution)/shard_map/pallas_call | solution.py:193
  46.4 3.7 %collective-permute-done.4.top_near = f32[32,24,128]{2,1,0:T(8,128)S(1)} collective-permute-done((f32[32,24,128]{2,1,0:T(8,128)S(1)}, f32[32,24,128]{2,1,0:T(8,128)S(1)}, u32[]{:S(2)}, u32[]{:S(2)}) %collective-permute-start.4) | collective-permute-done | bytes 393248 | tf_op jit(solution)/shard_map/ppermute | solution.py:209
  50.1 1.3 %collective-permute-done.5.low_near = f32[32,24,128]{2,1,0:T(8,128)S(1)} collective-permute-done((f32[32,24,128]{2,1,0:T(8,128)S(1)}, f32[32,24,128]{2,1,0:T(8,128)S(1)}, u32[]{:S(2)}, u32[]{:S(2)}) %collective-permute-start.5) | collective-permute-done | bytes 393248 | tf_op jit(solution)/shard_map/ppermute | solution.py:209
  51.5 8.4 %collective-permute-done.8.top_far = f32[32,24,128]{2,1,0:T(8,128)S(1)} collective-permute-done((f32[32,24,128]{2,1,0:T(8,128)S(1)}, f32[32,24,128]{2,1,0:T(8,128)S(1)}, u32[]{:S(2)}, u32[]{:S(2)}) %collective-permute-start.8) | collective-permute-done | bytes 393248 | tf_op jit(solution)/shard_map/ppermute | solution.py:209
  59.9 0.0 collective-permute-done.9.low_far
  59.9 1.0 shard_map.94
  60.9 0.0 all-to-all-done
  60.9 11.2 %all-to-all-start.1 = ((f32[64,24,128]{2,1,0:T(8,128)}), f32[64,24,128]{2,1,0:T(8,128)S(1)}, u32[]{:S(2)}, u32[]{:S(2)}) async-start(f32[64,24,128]{2,1,0:T(8,128)} %shard_map.94), calls=%async_computation.1 | async-start | bytes 1572864 | tf_op jit(solution)/shard_map/all_to_all | solution.py:212
  72.2 0.1 fusion
  72.3 0.1 convert_element_type.14.target
  72.3 2.3 %shard_map.96 = (f32[2056,128]{1,0:T(8,128)S(1)}, f32[1,128]{1,0:T(1,128)S(1)}) custom-call(s32[1024]{0:T(1024)S(1)} %convert_element_type.14.target), custom_call_target="tpu_custom_call" | custom-call | flops 262144 | bytes 1048576 | tf_op jit(solution)/shard_map/pallas_call | solution.py:253
  74.6 1.3 %shard_map.95.before = f32[2056,128]{1,0:T(8,128)S(1)} custom-call(s32[1024]{0:T(1024)S(1)} %convert_element_type.14.target, f32[640,128]{1,0:T(8,128)S(1)} %bitcast.25), custom_call_target="tpu_custom_call" | custom-call | flops 262144 | bytes 1048576 | tf_op jit(solution)/shard_map/pallas_call | solution.py:257
  75.9 19.2 %all-to-all-done.1 = f32[64,24,128]{2,1,0:T(8,128)S(1)} async-done(((f32[64,24,128]{2,1,0:T(8,128)}), f32[64,24,128]{2,1,0:T(8,128)S(1)}, u32[]{:S(2)}, u32[]{:S(2)}) %all-to-all-start.1) | async-done | bytes 786464 | tf_op jit(solution)/shard_map/all_to_all | solution.py:212
  95.1 2.4 %shard_map.97 = (f32[2056,128]{1,0:T(8,128)S(1)}, f32[256,128]{1,0:T(8,128)S(1)}) custom-call(s32[1024]{0:T(1024)S(1)} %convert_element_type.14.target, f32[1536,128]{1,0:T(8,128)S(1)} %bitcast.24, f32[2056,128]{1,0:T(8,128)S(1)} %shard_map.95.before, f32[1,128]{1,0:T(1,128)S(1)} %get-tuple-element.46.count), custom_call_target="tpu_custom_call" | custom-call | flops 262144 | bytes 1048576 | tf_op jit(solution)/shard_map/pallas_call | solution.py:260
  97.5 20.5 %all_to_all.15 = f32[256,1,128]{2,1,0:T(1,128)S(1)} all-to-all(f32[256,1,128]{2,1,0:T(1,128)S(1)} %bitcast.27), channel_id=1, replica_groups=mesh['grp'=4,'own_0'=4,'own_1'=8,'own_2'=2] {'grp','own_0','own_1','own_2'}, dimensions={0} | all-to-all | bytes 262144 | tf_op jit(solution)/shard_map/all_to_all | solution.py:267
  118.1 3.3 %shard_map.98 = (f32[2048,128]{1,0:T(8,128)}, f32[2048,128]{1,0:T(8,128)}, f32[2048,128]{1,0:T(8,128)}) custom-call(f32[256,128]{1,0:T(8,128)S(1)} %bitcast.26, f32[2056,128]{1,0:T(8,128)S(1)} %get-tuple-element.48.dense, f32[2056,128]{1,0:T(8,128)S(1)} %get-tuple-element.49.mask, f32[2048,128]{1,0:T(8,128)} %bitcast.34, f32[2048,128]{1,0:T(8,128)} %bitcast.35, ...), custom_call_target="tpu_custom_call" | custom-call | flops 262144 | bytes 1048576 | tf_op jit(solution)/shard_map/pallas_call | solution.py:272
  (3 shorter events, 0.0 us)
Async XLA Ops:
  0.6 10.1 %copy-start = (s32[1,4,64,16]{2,3,1,0:T(8,128)S(1)}, s32[1,4,64,16]{2,3,1,0:T(8,128)}, u32[]{:S(2)}) copy-start(s32[1,4,64,16]{2,3,1,0:T(8,128)} %param.7) | copy-start | bytes 49156
  2.4 9.2 %collective-permute-start = (f32[2,32,8,128]{3,2,1,0:T(8,128)S(1)}, f32[2,32,8,128]{3,2,1,0:T(8,128)S(1)}, u32[]{:S(2)}, u32[]{:S(2)}) collective-permute-start(f32[2,32,8,128]{3,2,1,0:T(8,128)S(1)} %get-tuple-element.30), channel_id=1, source_target_pairs={{0,64},{64,0},{128,192},{192,128},{1,65},{65,1},{129,193},{193,129... | collective-permute-start | bytes 786440 | tf_op jit(solution)/shard_map/ppermute | solution.py:209
  4.5 7.8 %collective-permute-start.1 = (f32[2,32,8,128]{3,2,1,0:T(8,128)S(1)}, f32[2,32,8,128]{3,2,1,0:T(8,128)S(1)}, u32[]{:S(2)}, u32[]{:S(2)}) collective-permute-start(f32[2,32,8,128]{3,2,1,0:T(8,128)S(1)} %get-tuple-element.31), channel_id=1, source_target_pairs={{0,192},{64,128},{128,64},{192,0},{1,193},{65,129},{129,65},{193,1... | collective-permute-start | bytes 786440 | tf_op jit(solution)/shard_map/ppermute | solution.py:209
  8.0 35.5 %collective-permute-start.6 = (f32[32,24,128]{2,1,0:T(8,128)S(1)}, f32[32,24,128]{2,1,0:T(8,128)S(1)}, u32[]{:S(2)}, u32[]{:S(2)}) collective-permute-start(f32[32,24,128]{2,1,0:T(8,128)S(1)} %get-tuple-element.42), channel_id=1, source_target_pairs={{0,64},{64,0},{128,192},{192,128},{1,65},{65,1},{129,193},{193,129... | collective-permute-start | bytes 1179656 | tf_op jit(solution)/shard_map/ppermute | solution.py:209
  8.4 35.1 %collective-permute-start.7 = (f32[32,24,128]{2,1,0:T(8,128)S(1)}, f32[32,24,128]{2,1,0:T(8,128)S(1)}, u32[]{:S(2)}, u32[]{:S(2)}) collective-permute-start(f32[32,24,128]{2,1,0:T(8,128)S(1)} %get-tuple-element.43), channel_id=1, source_target_pairs={{0,192},{64,128},{128,64},{192,0},{1,193},{65,129},{129,65},{193,1... | collective-permute-start | bytes 1179656 | tf_op jit(solution)/shard_map/ppermute | solution.py:209
  12.4 11.2 %collective-permute-start.2 = (f32[32,8,128]{2,1,0:T(8,128)S(1)}, f32[32,8,128]{2,1,0:T(8,128)S(1)}, u32[]{:S(2)}, u32[]{:S(2)}) collective-permute-start(f32[32,8,128]{2,1,0:T(8,128)S(1)} %get-tuple-element.34), channel_id=1, source_target_pairs={{0,192},{64,128},{128,64},{192,0},{1,193},{65,129},{129,65},{193,1... | collective-permute-start | bytes 393224 | tf_op jit(solution)/shard_map/ppermute | solution.py:209
  14.6 9.0 %collective-permute-start.3 = (f32[32,8,128]{2,1,0:T(8,128)S(1)}, f32[32,8,128]{2,1,0:T(8,128)S(1)}, u32[]{:S(2)}, u32[]{:S(2)}) collective-permute-start(f32[32,8,128]{2,1,0:T(8,128)S(1)} %get-tuple-element.35), channel_id=1, source_target_pairs={{0,64},{64,0},{128,192},{192,128},{1,65},{65,1},{129,193},{193,129... | collective-permute-start | bytes 393224 | tf_op jit(solution)/shard_map/ppermute | solution.py:209
  24.4 36.5 %all-to-all-start = ((f32[64,1,1280]{2,1,0:T(1,128)}), f32[64,1,1280]{2,1,0:T(1,128)S(1)}, u32[]{:S(2)}, u32[]{:S(2)}) async-start(f32[64,1,1280]{2,1,0:T(1,128)} %bitcast.7), calls=%async_computation | async-start | bytes 655360 | tf_op jit(solution)/shard_map/all_to_all | solution.py:212
  39.8 10.3 %collective-permute-start.4 = (f32[32,24,128]{2,1,0:T(8,128)S(1)}, f32[32,24,128]{2,1,0:T(8,128)S(1)}, u32[]{:S(2)}, u32[]{:S(2)}) collective-permute-start(f32[32,24,128]{2,1,0:T(8,128)S(1)} %get-tuple-element.38), channel_id=1, source_target_pairs={{0,64},{64,0},{128,192},{192,128},{1,65},{65,1},{129,193},{193,129... | collective-permute-start | bytes 1179656 | tf_op jit(solution)/shard_map/ppermute | solution.py:209
  39.9 11.5 %collective-permute-start.5 = (f32[32,24,128]{2,1,0:T(8,128)S(1)}, f32[32,24,128]{2,1,0:T(8,128)S(1)}, u32[]{:S(2)}, u32[]{:S(2)}) collective-permute-start(f32[32,24,128]{2,1,0:T(8,128)S(1)} %get-tuple-element.39), channel_id=1, source_target_pairs={{0,192},{64,128},{128,64},{192,0},{1,193},{65,129},{129,65},{193,1... | collective-permute-start | bytes 1179656 | tf_op jit(solution)/shard_map/ppermute | solution.py:209
  43.6 16.2 %collective-permute-start.8 = (f32[32,24,128]{2,1,0:T(8,128)S(1)}, f32[32,24,128]{2,1,0:T(8,128)S(1)}, u32[]{:S(2)}, u32[]{:S(2)}) collective-permute-start(f32[32,24,128]{2,1,0:T(8,128)S(1)} %get-tuple-element.44), channel_id=1, source_target_pairs={{0,192},{64,128},{128,64},{192,0},{1,193},{65,129},{129,65},{193,1... | collective-permute-start | bytes 1179656 | tf_op jit(solution)/shard_map/ppermute | solution.py:209
  44.6 15.3 %collective-permute-start.9 = (f32[32,24,128]{2,1,0:T(8,128)S(1)}, f32[32,24,128]{2,1,0:T(8,128)S(1)}, u32[]{:S(2)}, u32[]{:S(2)}) collective-permute-start(f32[32,24,128]{2,1,0:T(8,128)S(1)} %get-tuple-element.45), channel_id=1, source_target_pairs={{0,64},{64,0},{128,192},{192,128},{1,65},{65,1},{129,193},{193,129... | collective-permute-start | bytes 1179656 | tf_op jit(solution)/shard_map/ppermute | solution.py:209
  60.9 34.2 %all-to-all-start.1 = ((f32[64,24,128]{2,1,0:T(8,128)}), f32[64,24,128]{2,1,0:T(8,128)S(1)}, u32[]{:S(2)}, u32[]{:S(2)}) async-start(f32[64,24,128]{2,1,0:T(8,128)} %shard_map.94), calls=%async_computation.1 | async-start | bytes 1572864 | tf_op jit(solution)/shard_map/all_to_all | solution.py:212
